TPU v7x, 512 devices: a whole 4x4x16 slice. The times are simulated.
512 devices in a mesh: segment: 4 (over x), tx: 8 (over y, z_hi), ty: 16 (over z_lo, core).
Axes of the slice: x: 4, y: 4, z: 16 (z_hi: 2, z_lo: 8; z = z_hi * 8 + z_lo), core: 2. Of those that a mesh axis runs over, the one named last changes fastest.
Arguments:
- act_in: bfloat16 [4, 128, 1024, 128], P('segment', 'tx', 'ty'), may hold values from -6 to 6
- partner_in: bfloat16 [4, 128, 1024, 128], P('segment', 'tx', 'ty'), may hold values from -6 to 6
- stashed: bfloat16 [4, 128, 1024, 128], P('segment', 'tx', 'ty'), may hold values from -6 to 6
- grad_in: bfloat16 [4, 128, 1024, 128], P('segment', 'tx', 'ty'), may hold values from -6 to 6
- down_weights: bfloat16 [4, 3, 3, 128, 192], P('segment'), may hold values from -0.1875 to 0.1875
- up_weights: bfloat16 [4, 3, 3, 192, 128], P('segment'), may hold values from -0.15625 to 0.15625
- coarse: bfloat16 [8192, 128], P(('tx', 'ty')), may hold values from -6 to 6
- nest_owner: int32 [8192, 1], P(('tx', 'ty')), may hold values from 0 to 15; in each aligned block of 64 rows (0 to 63, 64 to 127, ...) at most 8 rows name the same one
- nest_cell: int32 [8192], P(('tx', 'ty')), may hold values from 0 to 63
- land_weight: int32 [32, 256], P('tx', 'ty'), may hold values from 1 to 4
Outputs:
- act_out: bfloat16 [4, 128, 1024, 128], P('segment', 'tx', 'ty')
- grad_out: bfloat16 [4, 128, 1024, 128], P('segment', 'tx', 'ty')
- partner_out: bfloat16 [4, 128, 1024, 128], P('segment', 'tx', 'ty')
- down_grads: float32 [4, 221184], P('segment', ('tx', 'ty'))
- up_grads: float32 [4, 221184], P('segment', ('tx', 'ty'))
Inputs may be any that keep to these rules, and one draw needn't show every extreme that they name: `nest_owner`: within the rows of one device (aligned blocks of 64 rows) no owner is named more than 8 times, a bound that some block reaches; every owner is named by some row.
All inputs are finite; a program needn't handle non-finite values.
Results may differ from a plain program's by a relative error of at most 0.0085.
Values may be sent and summed in bfloat16 or wider, within the bound.
A program may use at most 64 MiB of HBM per device.

v0:
```python
import math

import jax
import jax.numpy as jnp
from jax import lax
from jax.sharding import PartitionSpec as P


def padded_2(shard, sides, width):
    for axis, dim in sides:
        peers, length = (lax.axis_size(axis), shard.shape[dim])
        up = [(i, (i + 1) % peers) for i in range(peers - 1)]
        down = [(j, i) for i, j in up]
        last = lax.slice_in_dim(shard, length - width, length, axis=dim)
        leading = lax.slice_in_dim(shard, 0, width, axis=dim)
        before = lax.ppermute(last, axis, up)
        after = lax.ppermute(leading, axis, down)
        shard = jnp.concatenate([before, shard, after], axis=dim)
    return shard


def from_behind(block, axis, distance):
    devices = range(lax.axis_size(axis))
    route = [(i - distance, i) for i in devices if i - distance in devices]
    return lax.ppermute(block, axis, route)


def convolve(inputs, kernel, stride, padding, dilation):
    result = lax.conv_general_dilated(
        inputs[None],
        kernel,
        (stride, stride),
        padding,
        lhs_dilation=(dilation, dilation),
        dimension_numbers=("NHWC", "HWIO", "NHWC"),
        preferred_element_type=jnp.float32,
    )
    return result[0]


def flipped(kernel):
    return jnp.transpose(kernel[::-1, ::-1], (0, 1, 3, 2))


def enlarge(values, factor):
    return jnp.repeat(jnp.repeat(values, factor, axis=0), factor, axis=1)


def pooled(values):
    height, breadth, channels = values.shape
    return values.reshape(height // 2, 2, breadth // 2, 2, channels).sum(axis=(1, 3))


def silu_slope(preact):
    logistic = jax.nn.sigmoid(preact)
    return logistic * (1.0 + preact * (1.0 - logistic))


def kernel_grad(padded, cotangent, stride):
    height, breadth, channels = cotangent.shape
    flat_grad = cotangent.reshape(height * breadth, channels)
    pieces = []
    for row_tap in range(3):
        for col_tap in range(3):
            window = padded[
                row_tap : row_tap + stride * (height - 1) + 1 : stride,
                col_tap : col_tap + stride * (breadth - 1) + 1 : stride,
            ]
            window = window.reshape(height * breadth, window.shape[-1])
            pieces.append(
                lax.dot_general(
                    window, flat_grad, (((0,), (0,)), ((), ())), preferred_element_type=jnp.float32
                )
            )
    return jnp.stack(pieces).reshape(-1)


def with_rims(block_cells):
    return padded_2(block_cells, (("tx", 0), ("ty", 1)), 1)


def lower_parts(block_cells, down_kernel):
    input_rim = with_rims(block_cells)
    pre_down = convolve(input_rim, down_kernel, 2, "VALID", 1)
    reduced = jax.nn.silu(pre_down).astype(jnp.bfloat16)
    raised_rim = enlarge(with_rims(reduced), 2)[1:-1, 1:-1]
    return (input_rim, pre_down, raised_rim)


def fetch_condition(coarse, nest_owner, nest_cell):
    owners = lax.axis_size("ty")
    needed = nest_cell.shape[0]
    capacity = max(2, 2 * needed // owners)
    owner_ids = nest_owner[:, 0]
    one_hot = (owner_ids[:, None] == jnp.arange(owners, dtype=jnp.int32)[None, :]).astype(jnp.int32)
    earlier = jnp.cumsum(one_hot, axis=0) - one_hot
    slot_ids = jnp.sum(earlier * one_hot, axis=1)
    request = jnp.zeros((owners, capacity), jnp.int32).at[owner_ids, slot_ids].set(nest_cell)
    answered = coarse[lax.all_to_all(request, "ty", split_axis=0, concat_axis=0, tiled=True)]
    replies = lax.all_to_all(answered, "ty", split_axis=0, concat_axis=0, tiled=True)
    return replies[owner_ids, slot_ids]


def local(
    act_in,
    partner_in,
    stashed,
    grad_in,
    down_weights,
    up_weights,
    coarse,
    nest_owner,
    nest_cell,
    land_weight,
):
    segments = lax.axis_size("segment")
    position = lax.axis_index("segment")
    decoder = (position >= segments // 2).astype(jnp.float32)
    encoder = 1.0 - decoder
    last_segment = position == segments - 1
    height, breadth, channels = (act_in.shape[1], act_in.shape[2], act_in.shape[3])
    fetched = fetch_condition(coarse, nest_owner, nest_cell)
    condition = enlarge(fetched.reshape(height // 4, breadth // 4, channels), 4).astype(jnp.float32)
    down_kernel = down_weights[0]
    up_kernel = up_weights[0]
    scaling = 1.0 / math.sqrt(height * breadth * lax.axis_size("tx") * lax.axis_size("ty"))
    block_in = (
        act_in[0].astype(jnp.float32) + decoder * partner_in[0].astype(jnp.float32) + condition
    ).astype(jnp.bfloat16)
    input_rim, pre_down, raised_rim = lower_parts(block_in, down_kernel)
    output = (block_in.astype(jnp.float32) + convolve(raised_rim, up_kernel, 1, "VALID", 1)).astype(
        jnp.bfloat16
    )
    weighting = jnp.where(last_segment, enlarge(land_weight.astype(jnp.float32), 4), 1.0)
    out_grad = (
        (grad_in[0].astype(jnp.float32) + encoder * partner_in[0].astype(jnp.float32))
        * weighting[:, :, None]
    ).astype(jnp.bfloat16)
    back_rim, pre_back, raised_back = lower_parts(stashed[0], down_kernel)
    up_term = kernel_grad(raised_back, out_grad, 1) * scaling
    raised_grad = convolve(with_rims(out_grad), flipped(up_kernel), 1, "VALID", 1)
    pre_grad = (pooled(raised_grad) * silu_slope(pre_back)).astype(jnp.bfloat16)
    grad_rim = with_rims(pre_grad)[1:, 1:]
    in_grad = (
        out_grad.astype(jnp.float32)
        + convolve(grad_rim, flipped(down_kernel), 1, ((1, 0), (1, 0)), 2)
    ).astype(jnp.bfloat16)
    down_term = kernel_grad(back_rim, pre_grad, 2) * scaling
    up_sum, down_sum = (
        lax.psum_scatter(up_term, ("tx", "ty"), scatter_dimension=0, tiled=True),
        lax.psum_scatter(down_term, ("tx", "ty"), scatter_dimension=0, tiled=True),
    )
    from_before = from_behind(output, "segment", 1)
    from_after = from_behind(in_grad, "segment", -1)
    far_act = from_behind(output, "segment", segments - 1)
    far_grad = from_behind(in_grad, "segment", 1 - segments)
    from_partner = jnp.select(
        [position == 0, position == 1, position == 2], [far_grad, from_after, from_before], far_act
    )
    return (from_before[None], from_after[None], from_partner[None], down_sum[None], up_sum[None])


def solution(mesh):
    placed = (
        P("segment", "tx", "ty", None),
        P("segment", "tx", "ty", None),
        P("segment", "tx", "ty", None),
        P("segment", "tx", "ty", None),
        P("segment", None, None, None, None),
        P("segment", None, None, None, None),
        P(("tx", "ty"), None),
        P(("tx", "ty"), None),
        P(("tx", "ty")),
        P("tx", "ty"),
    )
    return jax.shard_map(
        local,
        mesh=mesh,
        in_specs=placed,
        out_specs=(
            P("segment", "tx", "ty", None),
            P("segment", "tx", "ty", None),
            P("segment", "tx", "ty", None),
            P("segment", ("tx", "ty")),
            P("segment", ("tx", "ty")),
        ),
        check_vma=False,
    )
```

profile of v0, /device:TPU:1, one launch (start us, length us, event | category | flops | bytes accessed | tf_op | source)
XLA Modules:
  0.0 563.0 jit_solution(18179859921326242691)
XLA Ops:
  7.2 0.8 fusion.85
  8.1 0.8 select_reduce_fusion
  8.9 0.7 fusion.106
  9.6 5.7 %scatter_fusion = s32[16,8]{0,1:T(8,128)S(1)} fusion(s32[16,8]{0,1:T(8,128)S(1)} %broadcast.96, s32[64]{0:T(128)S(1)} %get-tuple-element.24, s32[64]{0:T(128)} %param.18), kind=kCustom, calls=%fused_computation.2 | custom fusion | bytes 1280 | tf_op jit(solution)/shard_map/scatter | solution.py:98
  15.4 0.7 copy.110
  16.0 14.0 %all-to-all-start = ((s32[16,1,8]{2,1,0:T(1,128)}), s32[16,1,8]{2,1,0:T(1,128)S(1)}, u32[]{:S(2)}, u32[]{:S(2)}) async-start(s32[16,1,8]{2,1,0:T(1,128)} %copy.110), calls=%async_computation | async-start | bytes 16384 | tf_op jit(solution)/shard_map/all_to_all | solution.py:99
  30.1 8.0 %collective-permute-start.13 = (bf16[1,64,128]{2,1,0:T(8,128)(2,1)S(1)}, bf16[1,64,128]{2,1,0:T(8,128)(2,1)S(1)}, u32[]{:S(2)}, u32[]{:S(2)}) collective-permute-start(bf16[1,64,128]{2,1,0:T(8,128)(2,1)S(1)} %get-tuple-element.34), channel_id=1, source_target_pairs={{0,16},{16,32},{32,48},{48,64},{64,80},{80,96},{96,112},{1,17},{17... | collective-permute-start | bytes 49160 | tf_op jit(solution)/shard_map/ppermute | solution.py:16
  38.1 1.3 collective-permute-start.14
  39.4 2.5 slice.173
  41.9 2.5 slice.174
  44.4 2.5 slice.176
  46.9 2.5 slice.177
  49.7 1.5 collective-permute-done.14
  51.3 4.9 collective-permute-start.15
  56.3 1.9 collective-permute-start.16
  58.2 1.3 gather_fusion
  59.5 10.0 %all-to-all-start.1 = ((bf16[16,8,128]{2,1,0:T(8,128)(2,1)}), bf16[16,8,128]{2,1,0:T(8,128)(2,1)S(1)}, u32[]{:S(2)}, u32[]{:S(2)}) async-start(bf16[16,8,128]{2,1,0:T(8,128)(2,1)} %bitcast.6), calls=%async_computation.1 | async-start | bytes 65536 | tf_op jit(solution)/shard_map/all_to_all | solution.py:100
  70.2 2.5 slice.169
  73.6 0.7 copy-done.19
  74.7 0.8 copy.128
  75.5 3.9 all-to-all-done.1
  79.4 0.8 gather_fusion.1
  80.9 1.3 collective-permute-start.10
  82.2 12.7 %collective-permute-start.9 = (bf16[1,64,128]{2,0,1:T(2,128)(2,1)S(1)}, bf16[1,64,128]{2,0,1:T(2,128)(2,1)S(1)}, u32[]{:S(2)}, u32[]{:S(2)}) collective-permute-start(bf16[1,64,128]{2,0,1:T(2,128)(2,1)S(1)} %get-tuple-element.36), channel_id=1, source_target_pairs={{0,16},{16,32},{32,48},{48,64},{64,80},{80,96},{96,112},{1,17},{17... | collective-permute-start | bytes 49160 | tf_op jit(solution)/shard_map/ppermute | solution.py:16
  95.0 11.2 %collective-permute-start = (bf16[1,64,128]{2,0,1:T(2,128)(2,1)S(1)}, bf16[1,64,128]{2,0,1:T(2,128)(2,1)S(1)}, u32[]{:S(2)}, u32[]{:S(2)}) collective-permute-start(bf16[1,64,128]{2,0,1:T(2,128)(2,1)S(1)} %get-tuple-element.40), channel_id=1, source_target_pairs={{0,16},{16,32},{32,48},{48,64},{64,80},{80,96},{96,112},{1,17},{17... | collective-permute-start | bytes 49160 | tf_op jit(solution)/shard_map/ppermute | solution.py:16
  106.2 1.3 collective-permute-start.1
  107.5 3.5 collective-permute-start.11
  111.0 1.9 collective-permute-start.12
  113.0 6.6 %collective-permute-done.1 = bf16[1,64,128]{2,0,1:T(2,128)(2,1)S(1)} collective-permute-done((bf16[1,64,128]{2,0,1:T(2,128)(2,1)S(1)}, bf16[1,64,128]{2,0,1:T(2,128)(2,1)S(1)}, u32[]{:S(2)}, u32[]{:S(2)}) %collective-permute-start.1) | collective-permute-done | bytes 16416 | tf_op jit(solution)/shard_map/ppermute | solution.py:17
  120.2 5.3 collective-permute-start.2
  125.5 1.9 collective-permute-start.3
  127.9 1.0 convolution_select_fusion
  130.0 0.8 reduce_sum.22
  131.7 8.7 %collective-permute-start.23 = (bf16[1,32,192]{2,0,1:T(2,128)(2,1)}, bf16[1,32,192]{2,0,1:T(2,128)(2,1)}, u32[]{:S(2)}, u32[]{:S(2)}) collective-permute-start(bf16[1,32,192]{2,0,1:T(2,128)(2,1)} %get-tuple-element.46), channel_id=1, source_target_pairs={{0,16},{16,32},{32,48},{48,64},{64,80},{80,96},{96,112},{1,17},{17... | collective-permute-start | bytes 36872 | tf_op jit(solution)/shard_map/ppermute | solution.py:16
  140.4 1.3 collective-permute-start.24
  145.0 1.5 mul.65
  146.5 12.7 %collective-permute-start.17 = (bf16[1,32,192]{2,0,1:T(2,128)(2,1)S(1)}, bf16[1,32,192]{2,0,1:T(2,128)(2,1)S(1)}, u32[]{:S(2)}, u32[]{:S(2)}) collective-permute-start(bf16[1,32,192]{2,0,1:T(2,128)(2,1)S(1)} %copy-done.17), channel_id=1, source_target_pairs={{0,16},{16,32},{32,48},{48,64},{64,80},{80,96},{96,112},{1,17},{17... | collective-permute-start | bytes 36872 | tf_op jit(solution)/shard_map/ppermute | solution.py:16
  159.3 1.6 collective-permute-start.18
  160.9 0.9 maximum_bitcast_fusion
  162.7 12.7 %collective-permute-start.4 = (bf16[1,32,192]{2,0,1:T(2,128)(2,1)S(1)}, bf16[1,32,192]{2,0,1:T(2,128)(2,1)S(1)}, u32[]{:S(2)}, u32[]{:S(2)}) collective-permute-start(bf16[1,32,192]{2,0,1:T(2,128)(2,1)S(1)} %get-tuple-element.50), channel_id=1, source_target_pairs={{0,16},{16,32},{32,48},{48,64},{64,80},{80,96},{96,112},{1,17},{17... | collective-permute-start | bytes 36872 | tf_op jit(solution)/shard_map/ppermute | solution.py:16
  175.4 1.3 collective-permute-start.5
  176.8 0.7 pad_maximum_fusion.9
  177.5 5.0 collective-permute-start.25
  182.5 1.9 collective-permute-start.26
  184.5 1.9 collective-permute-start.19
  186.4 2.4 collective-permute-done.5
  188.9 6.7 %collective-permute-start.6 = (bf16[10,1,192]{2,0,1:T(8,128)(2,1)S(1)}, bf16[10,1,192]{2,0,1:T(8,128)(2,1)S(1)}, u32[]{:S(2)}, u32[]{:S(2)}) collective-permute-start(bf16[10,1,192]{2,0,1:T(8,128)(2,1)S(1)} %get-tuple-element.44), channel_id=1, source_target_pairs={{0,1},{1,2},{2,3},{3,4},{4,5},{5,6},{6,7},{7,8},{8,9},{9,10},{10,1... | collective-permute-start | bytes 11528 | tf_op jit(solution)/shard_map/ppermute | solution.py:16
  195.5 1.9 collective-permute-start.7
  198.6 1.3 collective-permute-start.20
  199.9 1.3 collective-permute-start.22
  201.2 0.9 pad_maximum_fusion.3
  206.5 1.0 broadcast_multiply_fusion
  209.7 1.3 convolution_select_fusion.2
  211.2 6.3 %collective-permute-start.21 = (bf16[16,64,128]{2,0,1:T(8,128)(2,1)S(1)}, bf16[16,64,128]{2,0,1:T(8,128)(2,1)S(1)}, u32[]{:S(2)}, u32[]{:S(2)}) collective-permute-start(bf16[16,64,128]{2,0,1:T(8,128)(2,1)S(1)} %fusion.48), channel_id=1, source_target_pairs={{0,384},{1,385},{2,386},{3,387},{4,388},{5,389},{6,390},{7,391},{8... | collective-permute-start | bytes 786440 | tf_op jit(solution)/shard_map/ppermute | solution.py:25
  217.4 1.3 collective-permute-start.8
  218.8 0.7 add_reduce_fusion
  221.5 1.3 dynamic-slice
  223.4 1.0 select_bitcast_fusion
  224.4 0.8 copy.155
  225.2 0.8 copy.154
  226.0 0.8 copy.153
  226.8 326.6 %all-reduce.5.cloned.1.call-done = (f32[221184]{0:T(1024)}, f32[221184]{0:T(1024)}) async-done(((f32[221184]{0:T(1024)}, f32[221184]{0:T(1024)}), (f32[221184]{0:T(1024)}, f32[221184]{0:T(1024)})) %all-reduce.5.cloned.1.call-update) | async-done | bytes 1769488
  553.4 0.8 dynamic-slice.1
  554.8 0.8 dynamic-slice.3
  (172 shorter events, 18.8 us)
Async XLA Ops:
  7.2 120.7 %copy-start = (bf16[1,3,3,192,128]{4,3,2,1,0:T(8,128)(2,1)S(1)}, bf16[1,3,3,192,128]{4,3,2,1,0:T(8,128)(2,1)}, u32[]{:S(2)}) copy-start(bf16[1,3,3,192,128]{4,3,2,1,0:T(8,128)(2,1)} %param.15) | copy-start | bytes 1327108
  7.2 22.9 %copy-start.1 = (bf16[1,16,64,128]{3,2,1,0:T(8,128)(2,1)S(1)}, bf16[1,16,64,128]{3,2,1,0:T(8,128)(2,1)}, u32[]{:S(2)}) copy-start(bf16[1,16,64,128]{3,2,1,0:T(8,128)(2,1)} %param.12) | copy-start | bytes 786436
  7.2 32.2 %copy-start.18 = (s32[4,16]{1,0:T(4,128)S(1)}, s32[4,16]{1,0:T(4,128)}, u32[]{:S(2)}) copy-start(s32[4,16]{1,0:T(4,128)} %param.19) | copy-start | bytes 772
  9.6 48.6 %copy-start.2 = (bf16[64,128]{1,0:T(8,128)(2,1)S(1)}, bf16[64,128]{1,0:T(8,128)(2,1)}, u32[]{:S(2)}) copy-start(bf16[64,128]{1,0:T(8,128)(2,1)} %param.16) | copy-start | bytes 49156
  16.0 33.4 %all-to-all-start = ((s32[16,1,8]{2,1,0:T(1,128)}), s32[16,1,8]{2,1,0:T(1,128)S(1)}, u32[]{:S(2)}, u32[]{:S(2)}) async-start(s32[16,1,8]{2,1,0:T(1,128)} %copy.110), calls=%async_computation | async-start | bytes 16384 | tf_op jit(solution)/shard_map/all_to_all | solution.py:99
  30.1 19.6 %collective-permute-start.13 = (bf16[1,64,128]{2,1,0:T(8,128)(2,1)S(1)}, bf16[1,64,128]{2,1,0:T(8,128)(2,1)S(1)}, u32[]{:S(2)}, u32[]{:S(2)}) collective-permute-start(bf16[1,64,128]{2,1,0:T(8,128)(2,1)S(1)} %get-tuple-element.34), channel_id=1, source_target_pairs={{0,16},{16,32},{32,48},{48,64},{64,80},{80,96},{96,112},{1,17},{17... | collective-permute-start | bytes 49160 | tf_op jit(solution)/shard_map/ppermute | solution.py:16
  38.1 13.2 %collective-permute-start.14 = (bf16[1,64,128]{2,1,0:T(8,128)(2,1)S(1)}, bf16[1,64,128]{2,1,0:T(8,128)(2,1)S(1)}, u32[]{:S(2)}, u32[]{:S(2)}) collective-permute-start(bf16[1,64,128]{2,1,0:T(8,128)(2,1)S(1)} %get-tuple-element.35), channel_id=1, source_target_pairs={{16,0},{32,16},{48,32},{64,48},{80,64},{96,80},{112,96},{17,1},{33... | collective-permute-start | bytes 49160 | tf_op jit(solution)/shard_map/ppermute | solution.py:17
  51.3 18.7 %collective-permute-start.15 = (bf16[18,1,128]{2,1,0:T(2,128)(2,1)S(1)}, bf16[18,1,128]{2,1,0:T(2,128)(2,1)S(1)}, u32[]{:S(2)}, u32[]{:S(2)}) collective-permute-start(bf16[18,1,128]{2,1,0:T(2,128)(2,1)S(1)} %get-tuple-element.32), channel_id=1, source_target_pairs={{0,1},{1,2},{2,3},{3,4},{4,5},{5,6},{6,7},{7,8},{8,9},{9,10},{10,1... | collective-permute-start | bytes 13832 | tf_op jit(solution)/shard_map/ppermute | solution.py:16
  56.3 13.8 %collective-permute-start.16 = (bf16[18,1,128]{2,1,0:T(2,128)(2,1)S(1)}, bf16[18,1,128]{2,1,0:T(2,128)(2,1)S(1)}, u32[]{:S(2)}, u32[]{:S(2)}) collective-permute-start(bf16[18,1,128]{2,1,0:T(2,128)(2,1)S(1)} %get-tuple-element.33), channel_id=1, source_target_pairs={{1,0},{2,1},{3,2},{4,3},{5,4},{6,5},{7,6},{8,7},{9,8},{10,9},{11,1... | collective-permute-start | bytes 13832 | tf_op jit(solution)/shard_map/ppermute | solution.py:17
  59.5 19.9 %all-to-all-start.1 = ((bf16[16,8,128]{2,1,0:T(8,128)(2,1)}), bf16[16,8,128]{2,1,0:T(8,128)(2,1)S(1)}, u32[]{:S(2)}, u32[]{:S(2)}) async-start(bf16[16,8,128]{2,1,0:T(8,128)(2,1)} %bitcast.6), calls=%async_computation.1 | async-start | bytes 65536 | tf_op jit(solution)/shard_map/all_to_all | solution.py:100
  69.6 483.8 %all-reduce.5.cloned.1.call-start = ((), (), s32[]{:S(2)}) async-start(), calls=%async_computation.2 | async-start | bytes 3538944
  73.3 1.0 copy-start.19
  73.3 1.0 copy-start.24
  74.3 6.0 %copy-start.4 = (bf16[1,16,64,128]{3,2,1,0:T(8,128)(2,1)S(1)}, bf16[1,16,64,128]{3,2,1,0:T(8,128)(2,1)}, u32[]{:S(2)}) copy-start(bf16[1,16,64,128]{3,2,1,0:T(8,128)(2,1)} %param.13) | copy-start | bytes 786436
  74.3 6.0 %copy-start.5 = (bf16[1,16,64,128]{3,2,1,0:T(8,128)(2,1)S(1)}, bf16[1,16,64,128]{3,2,1,0:T(8,128)(2,1)}, u32[]{:S(2)}) copy-start(bf16[1,16,64,128]{3,2,1,0:T(8,128)(2,1)} %param.11) | copy-start | bytes 786436
  74.3 6.0 %copy-start.6 = (bf16[1,16,64,128]{3,2,1,0:T(8,128)(2,1)S(1)}, bf16[1,16,64,128]{3,2,1,0:T(8,128)(2,1)}, u32[]{:S(2)}) copy-start(bf16[1,16,64,128]{3,2,1,0:T(8,128)(2,1)} %param.10) | copy-start | bytes 786436
  80.9 26.6 %collective-permute-start.10 = (bf16[1,64,128]{2,0,1:T(2,128)(2,1)S(1)}, bf16[1,64,128]{2,0,1:T(2,128)(2,1)S(1)}, u32[]{:S(2)}, u32[]{:S(2)}) collective-permute-start(bf16[1,64,128]{2,0,1:T(2,128)(2,1)S(1)} %get-tuple-element.37), channel_id=1, source_target_pairs={{16,0},{32,16},{48,32},{64,48},{80,64},{96,80},{112,96},{17,1},{33... | collective-permute-start | bytes 49160 | tf_op jit(solution)/shard_map/ppermute | solution.py:17
  82.2 25.3 %collective-permute-start.9 = (bf16[1,64,128]{2,0,1:T(2,128)(2,1)S(1)}, bf16[1,64,128]{2,0,1:T(2,128)(2,1)S(1)}, u32[]{:S(2)}, u32[]{:S(2)}) collective-permute-start(bf16[1,64,128]{2,0,1:T(2,128)(2,1)S(1)} %get-tuple-element.36), channel_id=1, source_target_pairs={{0,16},{16,32},{32,48},{48,64},{64,80},{80,96},{96,112},{1,17},{17... | collective-permute-start | bytes 49160 | tf_op jit(solution)/shard_map/ppermute | solution.py:16
  95.0 18.0 %collective-permute-start = (bf16[1,64,128]{2,0,1:T(2,128)(2,1)S(1)}, bf16[1,64,128]{2,0,1:T(2,128)(2,1)S(1)}, u32[]{:S(2)}, u32[]{:S(2)}) collective-permute-start(bf16[1,64,128]{2,0,1:T(2,128)(2,1)S(1)} %get-tuple-element.40), channel_id=1, source_target_pairs={{0,16},{16,32},{32,48},{48,64},{64,80},{80,96},{96,112},{1,17},{17... | collective-permute-start | bytes 49160 | tf_op jit(solution)/shard_map/ppermute | solution.py:16
  106.2 13.4 %collective-permute-start.1 = (bf16[1,64,128]{2,0,1:T(2,128)(2,1)S(1)}, bf16[1,64,128]{2,0,1:T(2,128)(2,1)S(1)}, u32[]{:S(2)}, u32[]{:S(2)}) collective-permute-start(bf16[1,64,128]{2,0,1:T(2,128)(2,1)S(1)} %get-tuple-element.41), channel_id=1, source_target_pairs={{16,0},{32,16},{48,32},{64,48},{80,64},{96,80},{112,96},{17,1},{33... | collective-permute-start | bytes 49160 | tf_op jit(solution)/shard_map/ppermute | solution.py:17
  107.5 19.9 %collective-permute-start.11 = (bf16[18,1,128]{2,0,1:T(8,128)(2,1)S(1)}, bf16[18,1,128]{2,0,1:T(8,128)(2,1)S(1)}, u32[]{:S(2)}, u32[]{:S(2)}) collective-permute-start(bf16[18,1,128]{2,0,1:T(8,128)(2,1)S(1)} %get-tuple-element.28), channel_id=1, source_target_pairs={{0,1},{1,2},{2,3},{3,4},{4,5},{5,6},{6,7},{7,8},{8,9},{9,10},{10,1... | collective-permute-start | bytes 13832 | tf_op jit(solution)/shard_map/ppermute | solution.py:16
  111.0 16.4 %collective-permute-start.12 = (bf16[18,1,128]{2,0,1:T(8,128)(2,1)S(1)}, bf16[18,1,128]{2,0,1:T(8,128)(2,1)S(1)}, u32[]{:S(2)}, u32[]{:S(2)}) collective-permute-start(bf16[18,1,128]{2,0,1:T(8,128)(2,1)S(1)} %get-tuple-element.29), channel_id=1, source_target_pairs={{1,0},{2,1},{3,2},{4,3},{5,4},{6,5},{7,6},{8,7},{9,8},{10,9},{11,1... | collective-permute-start | bytes 13832 | tf_op jit(solution)/shard_map/ppermute | solution.py:17
  113.0 14.9 %copy-start.8 = (bf16[1,64,128]{2,0,1:T(2,128)(2,1)}, bf16[1,64,128]{2,0,1:T(2,128)(2,1)S(1)}, u32[]{:S(2)}) copy-start(bf16[1,64,128]{2,0,1:T(2,128)(2,1)S(1)} %collective-permute-done) | copy-start | bytes 49156
  119.6 8.2 %copy-start.10 = (bf16[1,64,128]{2,0,1:T(2,128)(2,1)}, bf16[1,64,128]{2,0,1:T(2,128)(2,1)S(1)}, u32[]{:S(2)}) copy-start(bf16[1,64,128]{2,0,1:T(2,128)(2,1)S(1)} %collective-permute-done.1) | copy-start | bytes 49156
  120.2 39.0 %collective-permute-start.2 = (bf16[18,1,128]{2,0,1:T(8,128)(2,1)}, bf16[18,1,128]{2,0,1:T(8,128)(2,1)}, u32[]{:S(2)}, u32[]{:S(2)}) collective-permute-start(bf16[18,1,128]{2,0,1:T(8,128)(2,1)} %get-tuple-element.30), channel_id=1, source_target_pairs={{0,1},{1,2},{2,3},{3,4},{4,5},{5,6},{6,7},{7,8},{8,9},{9,10},{10,1... | collective-permute-start | bytes 13832 | tf_op jit(solution)/shard_map/ppermute | solution.py:16
  125.5 2.4 copy-start.21
  125.5 35.4 %collective-permute-start.3 = (bf16[18,1,128]{2,0,1:T(8,128)(2,1)}, bf16[18,1,128]{2,0,1:T(8,128)(2,1)}, u32[]{:S(2)}, u32[]{:S(2)}) collective-permute-start(bf16[18,1,128]{2,0,1:T(8,128)(2,1)} %get-tuple-element.31), channel_id=1, source_target_pairs={{1,0},{2,1},{3,2},{4,3},{5,4},{6,5},{7,6},{8,7},{9,8},{10,9},{11,1... | collective-permute-start | bytes 13832 | tf_op jit(solution)/shard_map/ppermute | solution.py:17
  130.0 1.0 copy-start.3
  130.0 12.4 %copy-start.7 = (bf16[8,32,128]{2,1,0:T(8,128)(2,1)S(1)}, bf16[8,32,128]{2,1,0:T(8,128)(2,1)}, u32[]{:S(2)}) copy-start(bf16[8,32,128]{2,1,0:T(8,128)(2,1)} %slice.169) | copy-start | bytes 196612
  130.8 12.5 %copy-start.15 = (bf16[8,32,128]{2,1,0:T(8,128)(2,1)S(1)}, bf16[8,32,128]{2,1,0:T(8,128)(2,1)}, u32[]{:S(2)}) copy-start(bf16[8,32,128]{2,1,0:T(8,128)(2,1)} %slice.173) | copy-start | bytes 196612
  130.9 12.6 %copy-start.14 = (bf16[8,32,128]{2,1,0:T(8,128)(2,1)S(1)}, bf16[8,32,128]{2,1,0:T(8,128)(2,1)}, u32[]{:S(2)}) copy-start(bf16[8,32,128]{2,1,0:T(8,128)(2,1)} %slice.174) | copy-start | bytes 196612
  131.7 12.3 %copy-start.13 = (bf16[8,32,128]{2,1,0:T(8,128)(2,1)S(1)}, bf16[8,32,128]{2,1,0:T(8,128)(2,1)}, u32[]{:S(2)}) copy-start(bf16[8,32,128]{2,1,0:T(8,128)(2,1)} %slice.176) | copy-start | bytes 196612
  131.7 43.7 %collective-permute-start.23 = (bf16[1,32,192]{2,0,1:T(2,128)(2,1)}, bf16[1,32,192]{2,0,1:T(2,128)(2,1)}, u32[]{:S(2)}, u32[]{:S(2)}) collective-permute-start(bf16[1,32,192]{2,0,1:T(2,128)(2,1)} %get-tuple-element.46), channel_id=1, source_target_pairs={{0,16},{16,32},{32,48},{48,64},{64,80},{80,96},{96,112},{1,17},{17... | collective-permute-start | bytes 36872 | tf_op jit(solution)/shard_map/ppermute | solution.py:16
  140.4 36.3 %collective-permute-start.24 = (bf16[1,32,192]{2,0,1:T(2,128)(2,1)}, bf16[1,32,192]{2,0,1:T(2,128)(2,1)}, u32[]{:S(2)}, u32[]{:S(2)}) collective-permute-start(bf16[1,32,192]{2,0,1:T(2,128)(2,1)} %get-tuple-element.47), channel_id=1, source_target_pairs={{16,0},{32,16},{48,32},{64,48},{80,64},{96,80},{112,96},{17,1},{33... | collective-permute-start | bytes 36872 | tf_op jit(solution)/shard_map/ppermute | solution.py:17
  142.6 1.6 copy-start.12
  144.9 1.6 copy-start.17
  144.9 14.3 %copy-start.16 = (bf16[1,32,192]{2,0,1:T(2,128)(2,1)S(1)}, bf16[1,32,192]{2,0,1:T(2,128)(2,1)}, u32[]{:S(2)}) copy-start(bf16[1,32,192]{2,0,1:T(2,128)(2,1)} %get-tuple-element.49) | copy-start | bytes 36868
  145.0 15.9 %copy-start.9 = (bf16[1,64,128]{2,0,1:T(2,128)(2,1)S(1)}, bf16[1,64,128]{2,0,1:T(2,128)(2,1)}, u32[]{:S(2)}) copy-start(bf16[1,64,128]{2,0,1:T(2,128)(2,1)} %copy-done.8) | copy-start | bytes 49156
  145.0 15.9 %copy-start.11 = (bf16[1,64,128]{2,0,1:T(2,128)(2,1)S(1)}, bf16[1,64,128]{2,0,1:T(2,128)(2,1)}, u32[]{:S(2)}) copy-start(bf16[1,64,128]{2,0,1:T(2,128)(2,1)} %copy-done.10) | copy-start | bytes 49156
  146.5 36.0 %collective-permute-start.17 = (bf16[1,32,192]{2,0,1:T(2,128)(2,1)S(1)}, bf16[1,32,192]{2,0,1:T(2,128)(2,1)S(1)}, u32[]{:S(2)}, u32[]{:S(2)}) collective-permute-start(bf16[1,32,192]{2,0,1:T(2,128)(2,1)S(1)} %copy-done.17), channel_id=1, source_target_pairs={{0,16},{16,32},{32,48},{48,64},{64,80},{80,96},{96,112},{1,17},{17... | collective-permute-start | bytes 36872 | tf_op jit(solution)/shard_map/ppermute | solution.py:16
  159.2 2.8 copy-start.20
  159.3 2.8 copy-start.25
  159.3 25.2 %collective-permute-start.18 = (bf16[1,32,192]{2,0,1:T(2,128)(2,1)S(1)}, bf16[1,32,192]{2,0,1:T(2,128)(2,1)S(1)}, u32[]{:S(2)}, u32[]{:S(2)}) collective-permute-start(bf16[1,32,192]{2,0,1:T(2,128)(2,1)S(1)} %copy-done.16), channel_id=1, source_target_pairs={{16,0},{32,16},{48,32},{64,48},{80,64},{96,80},{112,96},{17,1},{33... | collective-permute-start | bytes 36872 | tf_op jit(solution)/shard_map/ppermute | solution.py:17
  162.7 35.0 %copy-start.23 = (pred[8,10]{0,1:T(8,128)(4,1)S(1)}, pred[8,10]{0,1:T(8,128)(4,1)}, u32[]{:S(2)}) copy-start(pred[8,10]{0,1:T(8,128)(4,1)} %constant.78) | copy-start | bytes 244
  162.7 23.7 %collective-permute-start.4 = (bf16[1,32,192]{2,0,1:T(2,128)(2,1)S(1)}, bf16[1,32,192]{2,0,1:T(2,128)(2,1)S(1)}, u32[]{:S(2)}, u32[]{:S(2)}) collective-permute-start(bf16[1,32,192]{2,0,1:T(2,128)(2,1)S(1)} %get-tuple-element.50), channel_id=1, source_target_pairs={{0,16},{16,32},{32,48},{48,64},{64,80},{80,96},{96,112},{1,17},{17... | collective-permute-start | bytes 36872 | tf_op jit(solution)/shard_map/ppermute | solution.py:16
  175.4 13.4 %collective-permute-start.5 = (bf16[1,32,192]{2,0,1:T(2,128)(2,1)S(1)}, bf16[1,32,192]{2,0,1:T(2,128)(2,1)S(1)}, u32[]{:S(2)}, u32[]{:S(2)}) collective-permute-start(bf16[1,32,192]{2,0,1:T(2,128)(2,1)S(1)} %get-tuple-element.51), channel_id=1, source_target_pairs={{16,0},{32,16},{48,32},{64,48},{80,64},{96,80},{112,96},{17,1},{33... | collective-permute-start | bytes 36872 | tf_op jit(solution)/shard_map/ppermute | solution.py:17
  177.5 22.4 %collective-permute-start.25 = (bf16[10,1,192]{2,0,1:T(8,128)(2,1)S(1)}, bf16[10,1,192]{2,0,1:T(8,128)(2,1)S(1)}, u32[]{:S(2)}, u32[]{:S(2)}) collective-permute-start(bf16[10,1,192]{2,0,1:T(8,128)(2,1)S(1)} %get-tuple-element.42), channel_id=1, source_target_pairs={{0,1},{1,2},{2,3},{3,4},{4,5},{5,6},{6,7},{7,8},{8,9},{9,10},{10,1... | collective-permute-start | bytes 11528 | tf_op jit(solution)/shard_map/ppermute | solution.py:16
  182.5 18.7 %collective-permute-start.26 = (bf16[10,1,192]{2,0,1:T(8,128)(2,1)S(1)}, bf16[10,1,192]{2,0,1:T(8,128)(2,1)S(1)}, u32[]{:S(2)}, u32[]{:S(2)}) collective-permute-start(bf16[10,1,192]{2,0,1:T(8,128)(2,1)S(1)} %get-tuple-element.43), channel_id=1, source_target_pairs={{1,0},{2,1},{3,2},{4,3},{5,4},{6,5},{7,6},{8,7},{9,8},{10,9},{11,1... | collective-permute-start | bytes 11528 | tf_op jit(solution)/shard_map/ppermute | solution.py:17
  184.5 13.0 %collective-permute-start.19 = (bf16[10,1,192]{2,0,1:T(8,128)(2,1)S(1)}, bf16[10,1,192]{2,0,1:T(8,128)(2,1)S(1)}, u32[]{:S(2)}, u32[]{:S(2)}) collective-permute-start(bf16[10,1,192]{2,0,1:T(8,128)(2,1)S(1)} %pad_maximum_fusion.10), channel_id=1, source_target_pairs={{1,0},{2,1},{3,2},{4,3},{5,4},{6,5},{7,6},{8,7},{9,8},{10,9},{11,1... | collective-permute-start | bytes 11528 | tf_op jit(solution)/shard_map/ppermute | solution.py:17
  188.9 18.7 %collective-permute-start.6 = (bf16[10,1,192]{2,0,1:T(8,128)(2,1)S(1)}, bf16[10,1,192]{2,0,1:T(8,128)(2,1)S(1)}, u32[]{:S(2)}, u32[]{:S(2)}) collective-permute-start(bf16[10,1,192]{2,0,1:T(8,128)(2,1)S(1)} %get-tuple-element.44), channel_id=1, source_target_pairs={{0,1},{1,2},{2,3},{3,4},{4,5},{5,6},{6,7},{7,8},{8,9},{9,10},{10,1... | collective-permute-start | bytes 11528 | tf_op jit(solution)/shard_map/ppermute | solution.py:16
  195.5 12.0 %collective-permute-start.7 = (bf16[10,1,192]{2,0,1:T(8,128)(2,1)S(1)}, bf16[10,1,192]{2,0,1:T(8,128)(2,1)S(1)}, u32[]{:S(2)}, u32[]{:S(2)}) collective-permute-start(bf16[10,1,192]{2,0,1:T(8,128)(2,1)S(1)} %get-tuple-element.45), channel_id=1, source_target_pairs={{1,0},{2,1},{3,2},{4,3},{5,4},{6,5},{7,6},{8,7},{9,8},{10,9},{11,1... | collective-permute-start | bytes 11528 | tf_op jit(solution)/shard_map/ppermute | solution.py:17
  198.6 24.8 %collective-permute-start.20 = (bf16[16,64,128]{2,0,1:T(8,128)(2,1)S(1)}, bf16[16,64,128]{2,0,1:T(8,128)(2,1)S(1)}, u32[]{:S(2)}, u32[]{:S(2)}) collective-permute-start(bf16[16,64,128]{2,0,1:T(8,128)(2,1)S(1)} %fusion.46), channel_id=1, source_target_pairs={{128,0},{256,128},{384,256},{129,1},{257,129},{385,257},{130,2},{2... | collective-permute-start | bytes 786440 | tf_op jit(solution)/shard_map/ppermute | solution.py:25
  199.9 23.5 %collective-permute-start.22 = (bf16[16,64,128]{2,0,1:T(8,128)(2,1)S(1)}, bf16[16,64,128]{2,0,1:T(8,128)(2,1)}, u32[]{:S(2)}, u32[]{:S(2)}) collective-permute-start(bf16[16,64,128]{2,0,1:T(8,128)(2,1)S(1)} %fusion.46), channel_id=1, source_target_pairs={{384,0},{385,1},{386,2},{387,3},{388,4},{389,5},{390,6},{391,7},{3... | collective-permute-start | bytes 786440 | tf_op jit(solution)/shard_map/ppermute | solution.py:25
  209.0 0.7 copy-start.22
  211.2 12.2 %collective-permute-start.21 = (bf16[16,64,128]{2,0,1:T(8,128)(2,1)S(1)}, bf16[16,64,128]{2,0,1:T(8,128)(2,1)S(1)}, u32[]{:S(2)}, u32[]{:S(2)}) collective-permute-start(bf16[16,64,128]{2,0,1:T(8,128)(2,1)S(1)} %fusion.48), channel_id=1, source_target_pairs={{0,384},{1,385},{2,386},{3,387},{4,388},{5,389},{6,390},{7,391},{8... | collective-permute-start | bytes 786440 | tf_op jit(solution)/shard_map/ppermute | solution.py:25
  217.4 6.0 %collective-permute-start.8 = (bf16[16,64,128]{2,0,1:T(8,128)(2,1)S(1)}, bf16[16,64,128]{2,0,1:T(8,128)(2,1)S(1)}, u32[]{:S(2)}, u32[]{:S(2)}) collective-permute-start(bf16[16,64,128]{2,0,1:T(8,128)(2,1)S(1)} %fusion.48), channel_id=1, source_target_pairs={{0,128},{128,256},{256,384},{1,129},{129,257},{257,385},{2,130},{1... | collective-permute-start | bytes 786440 | tf_op jit(solution)/shard_map/ppermute | solution.py:25
Sparse Core Ops, SparseCore 0:
  209.2 344.1 all-reduce.4
where the time goes:
time: 564 us; the launch traced here: 563 us
  waiting for transfers between devices  341 us (60%)
  starting transfers between devices  145 us (26%)
  local copies, waits for them, and re-layouts  39 us (7%)
  between operations  18 us (3%)
  other arithmetic  10.9 us (2%)
  matrix products  8.71 us (2%)
    unnamed x2, waiting for transfers between devices  327 us
    ppermute x11, starting transfers between devices, padded_2(): before = lax.ppermute(last, axis, up)  91.4 us
    ppermute x12, starting transfers between devices, padded_2(): after = lax.ppermute(leading, axis, down)  19.6 us
    all_to_all x1, starting transfers between devices, fetch_condition(): lax.all_to_all(request, 'ty', split_axis=0, concat_axis=0, tiled=True)  14 us
    slice x9, local copies, waits for them, and re-layouts, kernel_grad(): padded[row_tap:row_tap + stride * (height - 1) + 1:stride, col_tap:col_ta...  13.4 us
  transfers between devices with their start and end apart: 30, of which 5 were waited for; matrix products, arithmetic and copies ran while one was open for 8% of the time, Pallas kernels for 0%

commit v1 on v0

v1 whole, which is shorter than its diff:
```python
import functools
import math

import jax
import jax.numpy as jnp
from jax import lax
from jax.experimental import pallas as pl
from jax.experimental.pallas import tpu as pltpu
from jax.sharding import PartitionSpec as P

F32 = jnp.float32
BF = jnp.bfloat16
MESH = pl.DeviceIdType.MESH

HT, WT, C, C2 = 16, 64, 128, 192
CP = 256
H2, W2 = HT // 2, WT // 2
M2 = H2 * W2
CELLS, CAP = 64, 8
NSEG, NTX, NTY = 4, 8, 16
NY, NZ = 4, 16
ROWS = 1728
QUART = ROWS // NY
PIECE = QUART // NZ
PADP = 32
TAPS_OF = ((2,), (1, 2), (0, 1), (0,))


def dot(a, b, dims=((1,), (0,))):
    return lax.dot_general(a, b, (dims, ((), ())), preferred_element_type=F32)


def rows_of(view, index):
    lanes = view.shape[-1]
    pairs = view.reshape(view.shape[0] // 2, 2, W2, lanes)
    start = index // 2
    return pairs[start : start + H2, index % 2].reshape(M2, lanes)


def kernel(
    act, par, sta, gra, dw, uw, coarse, nown, ncell, land,
    left_out, right_out, down_out, up_out,
    dwp, uc, t32, g32, soo, see, goo, gee, dim, wim,
    prb, pgf, rpf, r32, pw, gds, gf, gs, zs, zp, fs,
    pay_ig, pay_out,
    rqs, rqr, rps, rpr, condb, tr,
    srow_s, ogup_s, colr_s, coll_s,
    top_r, bot_r, lft_r, rgt_r, ctl_r, ctr_r, cbl_r, cbr_r,
    pgrow_s, pgcol_s, pgrow_r, pgcol_r, pgcor_r,
    birow_s, bicol_s, birow_r, bicol_r, bicor_r,
    rdt_s, rdb_s, rdl_s, rdr_s,
    rdt_r, rdb_r, rdl_r, rdr_r, rtl_r, rtr_r, rbl_r, rbr_r,
    gb, ra, yb, ry, zb, rz, fin, rfin,
    ssem, rsem,
):
    seg, tx, ty = lax.axis_index("segment"), lax.axis_index("tx"), lax.axis_index("ty")
    core = lax.rem(ty, 2)
    zl = ty // 2
    zh = lax.rem(tx, 2)
    yy = tx // 2
    zz = zh * 8 + zl

    def at(dx, dy):
        return (seg, lax.rem(tx + dx + NTX, NTX), lax.rem(ty + dy + NTY, NTY))

    def ty_peer(q):
        return (seg, tx, lax.rem(ty + q, NTY))

    def y_peer(q):
        return (seg, lax.rem(yy + q, NY) * 2 + zh, ty)

    def z_peer(q):
        z = lax.rem(zz + q, NZ)
        return (seg, yy * 2 + z // 8, lax.rem(z, 8) * 2 + core)

    sibling = (seg, tx, zl * 2 + 1 - core)
    seg_next = (lax.rem(seg + 1, NSEG), tx, ty)
    seg_prev = (lax.rem(seg + NSEG - 1, NSEG), tx, ty)

    barrier = pltpu.get_barrier_semaphore()
    around = [(1, 0), (-1, 0), (0, 1), (0, -1), (1, 1), (1, -1), (-1, 1), (-1, -1)]
    greeted = [ty_peer(q) for q in range(1, NTY)]
    greeted += [at(dx, dy) for dx, dy in around if dx != 0]
    greeted += [y_peer(q) for q in range(1, NY)]
    greeted += [z_peer(q) for q in range(1, NZ)]
    greeted += [seg_next, seg_prev]
    for device in greeted:
        pl.semaphore_signal(barrier, inc=1, device_id=device, device_id_type=MESH)

    count = [0]
    started = []

    def slot():
        count[0] += 1
        return count[0] - 1

    def make(index, src, dst, device):
        return pltpu.make_async_remote_copy(
            src_ref=src, dst_ref=dst, send_sem=ssem.at[index], recv_sem=rsem.at[index],
            device_id=device, device_id_type=MESH,
        )

    def send(src, dst, device):
        copy = make(slot(), src, dst, device)
        copy.start()
        started.append(copy)
        return copy

    not_top, not_bottom = tx > 0, tx < NTX - 1
    not_left, not_right = ty > 0, ty < NTY - 1

    def keep(flag, value):
        return jnp.where(flag, value, 0.0)

    decoder = (seg >= NSEG // 2).astype(F32)
    encoder = 1.0 - decoder

    def iota(shape, axis):
        return lax.broadcasted_iota(jnp.int32, shape, axis)

    ocol = nown[...].astype(F32)
    crow = ncell[...].astype(F32)
    n0, n1 = iota((CELLS, CELLS), 0), iota((CELLS, CELLS), 1)
    orow = jnp.sum(jnp.where(n0 == n1, ocol, 0.0), axis=0, keepdims=True)
    ccol = jnp.sum(jnp.where(n0 == n1, crow, 0.0), axis=1, keepdims=True)
    same = jnp.where(ocol == orow, 1.0, 0.0)
    slot_row = jnp.sum(jnp.where(n0 < n1, same, 0.0), axis=0, keepdims=True)
    slot_col = jnp.sum(jnp.where(n1 < n0, same, 0.0), axis=1, keepdims=True)
    tyf = ty.astype(F32)

    def place(owner, slots):
        offset = owner - tyf
        return jnp.where(offset < 0.0, offset + NTY, offset) * CAP + slots

    qrow, qcol = place(orow, slot_row), place(ocol, slot_col)
    chosen = jnp.where(iota((NTY * CAP, CELLS), 0).astype(F32) == qrow, 1.0, 0.0).astype(BF)
    cell_hot = jnp.where(ccol == iota((CELLS, 128), 1).astype(F32), 1.0, 0.0).astype(BF)
    asked = dot(chosen, cell_hot)
    for q in range(NTY):
        rqs[q] = asked[q * CAP : (q + 1) * CAP].astype(BF)
    rqr[0] = rqs[0]

    spread = iota((WT, WT // 4), 1) == (iota((WT, WT // 4), 0) >> 2)
    for k in range(HT // 4):
        row = land[k : k + 1, :].astype(F32)
        weight = jnp.sum(jnp.where(spread, row, 0.0), axis=1, keepdims=True)
        weight = jnp.where(seg == NSEG - 1, weight, 1.0)
        for y in range(4 * k, 4 * k + 4):
            part = pl.ds(y * WT, WT)
            value = (gra[part, :].astype(F32) + encoder * par[part, :].astype(F32)) * weight
            g32[part, :] = value.astype(BF).astype(F32)
    t32[...] = sta[...].astype(F32)

    last = (HT - 1) * WT
    srow_s[0] = sta[last : last + WT, :]
    srow_s[1] = g32[last : last + WT, :].astype(BF)
    ogup_s[...] = g32[0:WT, :].astype(BF)
    colr_s[0] = t32[pl.ds(WT - 1, HT, stride=WT), :].astype(BF)
    colr_s[1] = g32[pl.ds(WT - 1, HT, stride=WT), :].astype(BF)
    coll_s[...] = g32[pl.ds(0, HT, stride=WT), :].astype(BF)

    pl.semaphore_wait(barrier, len(greeted))

    request = [send(rqs.at[q], rqr.at[q], ty_peer(q)) for q in range(1, NTY)]
    rim = [
        send(srow_s, top_r, at(1, 0)),
        send(ogup_s, bot_r, at(-1, 0)),
        send(colr_s, ctl_r, at(1, 1)),
        send(coll_s, ctr_r, at(1, -1)),
        send(colr_s.at[1], cbl_r, at(-1, 1)),
        send(coll_s, cbr_r, at(-1, -1)),
        send(colr_s, lft_r, at(0, 1)),
        send(coll_s, rgt_r, at(0, -1)),
    ]

    dwp[:, 0:C2] = dw[...]
    dwp[:, C2:CP] = jnp.zeros((9 * C, CP - C2), BF)
    uc[C2:CP, :] = jnp.zeros((CP - C2, 16 * C), BF)
    for u in range(4):
        for v in range(4):
            total = None
            for a in TAPS_OF[u]:
                for b in TAPS_OF[v]:
                    tap = uw[a * 3 + b].astype(F32)
                    total = tap if total is None else total + tap
            block = (u * 4 + v) * C
            uc[0:C2, block : block + C] = total.astype(BF)

    def fill(oo, ee, fine):
        ee[1:17, 0:W2, :] = fine[pl.ds(0, HT * W2, stride=2), :].reshape(HT, W2, C)
        oo[1:17, 8:40, :] = fine[pl.ds(1, HT * W2, stride=2), :].reshape(HT, W2, C)

    def fill_row(oo, ee, r, flag, row):
        tr[...] = keep(flag, row.astype(F32))
        ee[r, 0:W2, :] = tr[pl.ds(0, W2, stride=2), :]
        oo[r, 8:40, :] = tr[pl.ds(1, W2, stride=2), :]

    def fill_col(plane, first, at_col, flag, column):
        values = keep(flag, column.astype(F32))
        for r in range(values.shape[0]):
            plane[first + r, at_col : at_col + 1, :] = values[r : r + 1, :]

    def fill_cell(plane, r, at_col, flag, column, i):
        values = keep(flag, column.astype(F32))
        plane[r, at_col : at_col + 1, :] = values[i : i + 1, :]

    def put_half(value):
        r32[0] = value[:, 0:C]
        r32[1] = value[:, C:CP]

    def half_col(j):
        halves = [r32[h, pl.ds(j, H2, stride=W2), :] for h in range(2)]
        return jnp.concatenate(halves, axis=1).astype(BF)

    def gather_down(oo, ee):
        views = [oo[:, 7:39, :], ee[:, 0:32, :], oo[:, 8:40, :]]
        for b, view in enumerate(views):
            view = view.astype(BF)
            for a in range(3):
                block = (a * 3 + b) * C
                dim[:, block : block + C] = rows_of(view, a)

    fill(soo, see, t32)
    fill(goo, gee, g32)

    for copy in request:
        copy.wait_recv()
    wanted = jnp.concatenate([rqr[q].astype(F32) for q in range(NTY)], axis=0)
    answer = dot(wanted[:, 0:CELLS].astype(BF), coarse[...])
    for q in range(NTY):
        rps[q] = answer[q * CAP : (q + 1) * CAP].astype(BF)
    rpr[0] = rps[0]
    reply = [
        send(rps.at[q], rpr.at[q], (seg, tx, lax.rem(ty + NTY - q, NTY))) for q in range(1, NTY)
    ]

    for copy in rim:
        copy.wait_recv()
    fill_row(soo, see, 0, not_top, top_r[0])
    fill_row(goo, gee, 0, not_top, top_r[1])
    fill_row(goo, gee, 17, not_bottom, bot_r[...])
    fill_col(soo, 1, 7, not_left, lft_r[0])
    fill_col(goo, 1, 7, not_left, lft_r[1])
    fill_col(gee, 1, W2, not_right, rgt_r[...])
    fill_cell(soo, 0, 7, not_top & not_left, ctl_r[0], HT - 1)
    fill_cell(goo, 0, 7, not_top & not_left, ctl_r[1], HT - 1)
    fill_cell(gee, 0, W2, not_top & not_right, ctr_r[...], HT - 1)
    fill_cell(goo, 17, 7, not_bottom & not_left, cbl_r[...], 0)
    fill_cell(gee, 17, W2, not_bottom & not_right, cbr_r[...], 0)

    gather_down(soo, see)
    for v, view in enumerate([goo[:, 7:39, :], gee[:, 0:32, :], goo[:, 8:40, :], gee[:, 1:33, :]]):
        view = view.astype(BF)
        for u in range(4):
            block = (u * 4 + v) * C
            wim[:, block : block + C] = rows_of(view, u)

    pre_back = dot(dim[...], dwp[...])
    gate = jax.nn.sigmoid(pre_back)
    prb[...] = (pre_back * gate).astype(BF)
    pooled = dot(wim[...], uc[...], ((1,), (1,)))
    pre_grad = (pooled * (gate * (1.0 + pre_back * (1.0 - gate)))).astype(BF)
    half_grid = pre_grad.astype(F32)
    put_half(half_grid)
    pgrow_s[...] = half_grid[0:W2].astype(BF)
    pgcol_s[...] = half_col(0)
    pg_rim = [
        send(pgrow_s, pgrow_r, at(-1, 0)),
        send(pgcol_s, pgcor_r, at(-1, -1)),
        send(pgcol_s, pgcol_r, at(0, -1)),
    ]
    pgf[0:H2, 0:W2, :] = half_grid.reshape(H2, W2, CP)

    for copy in reply:
        copy.wait_recv()
    table = jnp.concatenate([rpr[q].astype(F32) for q in range(NTY)], axis=0).astype(BF)
    pick = jnp.where(iota((CELLS, NTY * CAP), 1).astype(F32) == qcol, 1.0, 0.0).astype(BF)
    fetched = dot(pick, table).astype(BF)
    r0, r1 = iota((4 * WT, CELLS), 0), iota((4 * WT, CELLS), 1)
    widen = jnp.where(r1 == ((r0 >> 6) << 4) + ((r0 & 63) >> 2), 1.0, 0.0).astype(BF)
    condb[...] = dot(widen, fetched)
    for y in range(HT):
        part = pl.ds(y * WT, WT)
        value = (
            act[part, :].astype(F32)
            + decoder * par[part, :].astype(F32)
            + condb[pl.ds(y // 4 * WT, WT), :]
        )
        t32[part, :] = value.astype(BF).astype(F32)
    birow_s[...] = t32[last : last + WT, :].astype(BF)
    bicol_s[...] = t32[pl.ds(WT - 1, HT, stride=WT), :].astype(BF)
    bi_rim = [
        send(birow_s, birow_r, at(1, 0)),
        send(bicol_s, bicor_r, at(1, 1)),
        send(bicol_s, bicol_r, at(0, 1)),
    ]
    fill(soo, see, t32)

    product = dot(dim[...], pre_grad, ((0,), (0,)))
    gds[0] = product[:, 0:C]
    gds[1] = product[:, C:CP]
    pw[...] = dot(prb[...], wim[...], ((0,), (0,)))
    low = iota((ROWS // 3, C), 1) < 64
    even_lo = gds[0, pl.ds(0, ROWS // 3, stride=2), :]
    even_hi = gds[1, pl.ds(0, ROWS // 3, stride=2), :]
    odd_lo = pltpu.roll(gds[0, pl.ds(1, ROWS // 3, stride=2), :], 64, 1)
    odd_hi = pltpu.roll(gds[1, pl.ds(1, ROWS // 3, stride=2), :], 64, 1)
    gf[0, pl.ds(0, ROWS // 3, stride=3), :] = even_lo
    gf[0, pl.ds(1, ROWS // 3, stride=3), :] = jnp.where(low, even_hi, odd_lo)
    gf[0, pl.ds(2, ROWS // 3, stride=3), :] = jnp.where(low, odd_lo, odd_hi)
    for a in range(3):
        for b in range(3):
            total = None
            for u in (2 - a, 3 - a):
                for v in (2 - b, 3 - b):
                    block = (u * 4 + v) * C
                    term = pw[0:C2, block : block + C]
                    total = term if total is None else total + term
            tap = (a * 3 + b) * C2
            gf[1, tap : tap + C2, :] = total
    gb[...] = gf[1 - core].astype(BF)
    swap = send(gb, ra, sibling)

    for copy in pg_rim:
        copy.wait_recv()
    pgf[H2, 0:W2, :] = keep(not_bottom, pgrow_r[...].astype(F32))
    fill_col(pgf, 0, W2, not_right, pgcol_r[...])
    fill_cell(pgf, H2, W2, not_bottom & not_right, pgcor_r[...], 0)
    shifted = [
        [pgf[di : di + H2, dj : dj + W2, :].astype(BF).reshape(M2, CP) for dj in (0, 1)]
        for di in (0, 1)
    ]

    def spread_out(value, pr, pc):
        for i in range(H2):
            t32[pl.ds((2 * i + pr) * WT + pc, W2, stride=2), :] = value[i * W2 : (i + 1) * W2]

    for pr in range(2):
        for pc in range(2):
            plane = gee[:, 0:32, :] if pc == 0 else goo[:, 8:40, :]
            value = rows_of(plane, 1 + pr)
            for a, di in ((1, 0),) if pr == 0 else ((2, 0), (0, 1)):
                for b, dj in ((1, 0),) if pc == 0 else ((2, 0), (0, 1)):
                    tap = (a * 3 + b) * C
                    value = value + dot(shifted[di][dj], dwp[tap : tap + C, :], ((1,), (1,)))
            spread_out(value, pr, pc)
    pay_ig[...] = t32[...].astype(BF)

    up_slot, down_slot = slot(), slot()
    ig_next = make(up_slot, pay_ig, left_out, seg_next)
    ig_prev = make(down_slot, pay_ig, right_out, seg_prev)
    out_next = make(up_slot, pay_out, left_out, seg_next)
    out_prev = make(down_slot, pay_out, right_out, seg_prev)

    @pl.when(seg == NSEG - 1)
    def _():
        ig_next.start()

    @pl.when(seg >= 1)
    def _():
        ig_prev.start()

    for copy in bi_rim:
        copy.wait_recv()
    fill_row(soo, see, 0, not_top, birow_r[...])
    fill_col(soo, 1, 7, not_left, bicol_r[...])
    fill_cell(soo, 0, 7, not_top & not_left, bicor_r[...], HT - 1)
    gather_down(soo, see)
    pre_down = dot(dim[...], dwp[...])
    half_grid = (pre_down * jax.nn.sigmoid(pre_down)).astype(BF).astype(F32)
    put_half(half_grid)
    rdt_s[...] = half_grid[0:W2].astype(BF)
    rdb_s[...] = half_grid[M2 - W2 : M2].astype(BF)
    rdl_s[...] = half_col(0)
    rdr_s[...] = half_col(W2 - 1)
    red_rim = [
        send(rdb_s, rdt_r, at(1, 0)),
        send(rdt_s, rdb_r, at(-1, 0)),
        send(rdr_s, rtl_r, at(1, 1)),
        send(rdl_s, rtr_r, at(1, -1)),
        send(rdr_s, rbl_r, at(-1, 1)),
        send(rdl_s, rbr_r, at(-1, -1)),
        send(rdr_s, rdl_r, at(0, 1)),
        send(rdl_s, rdr_r, at(0, -1)),
    ]
    rpf[1 : H2 + 1, 8:40, :] = half_grid.reshape(H2, W2, CP)

    swap.wait_recv()
    gs[...] = gf[core] + ra[...].astype(F32)
    yb[...] = gs[...].astype(BF).reshape(NY, QUART, C)
    y_sum = [send(yb.at[lax.rem(yy + q, NY)], ry.at[q - 1], y_peer(q)) for q in range(1, NY)]

    for copy in red_rim:
        copy.wait_recv()
    rpf[0, 8:40, :] = keep(not_top, rdt_r[...].astype(F32))
    rpf[H2 + 1, 8:40, :] = keep(not_bottom, rdb_r[...].astype(F32))
    fill_col(rpf, 1, 7, not_left, rdl_r[...])
    fill_col(rpf, 1, 40, not_right, rdr_r[...])
    fill_cell(rpf, 0, 7, not_top & not_left, rtl_r[...], H2 - 1)
    fill_cell(rpf, 0, 40, not_top & not_right, rtr_r[...], H2 - 1)
    fill_cell(rpf, H2 + 1, 7, not_bottom & not_left, rbl_r[...], 0)
    fill_cell(rpf, H2 + 1, 40, not_bottom & not_right, rbr_r[...], 0)
    moved = {}
    for dj in range(3):
        view = rpf[:, 7 + dj : 39 + dj, :].astype(BF)
        for di in range(3):
            moved[di, dj] = view[di : di + H2].reshape(M2, CP)
    meets = (((0, 3), (1, 1)), ((1, 2), (2, 0)))
    for pr in range(2):
        for pc in range(2):
            plane = see[:, 0:32, :] if pc == 0 else soo[:, 8:40, :]
            value = rows_of(plane, 1 + pr)
            for di, u in meets[pr]:
                for dj, v in meets[pc]:
                    block = (u * 4 + v) * C
                    value = value + dot(moved[di, dj], uc[:, block : block + C])
            spread_out(value, pr, pc)
    pay_out[...] = t32[...].astype(BF)

    @pl.when(seg <= NSEG - 2)
    def _():
        out_next.start()

    @pl.when(seg == 0)
    def _():
        out_prev.start()

    for copy in y_sum:
        copy.wait_recv()
    total = gs[pl.ds(yy * QUART, QUART), :]
    for q in range(NY - 1):
        total = total + ry[q].astype(F32)
    zs[0:QUART, :] = total
    zs[QUART:, :] = jnp.zeros((zs.shape[0] - QUART, C), F32)
    for z in range(NZ):
        zp[z] = zs[z * PIECE : z * PIECE + PADP, :]
    zb[...] = zp[...].astype(BF)
    z_sum = [send(zb.at[lax.rem(zz + q, NZ)], rz.at[q - 1], z_peer(q)) for q in range(1, NZ)]
    for copy in z_sum:
        copy.wait_recv()
    total = zp[zz]
    for q in range(NZ - 1):
        total = total + rz[q].astype(F32)
    scaling = 1.0 / math.sqrt(HT * WT * NTX * NTY)
    fin[...] = total * scaling
    last_swap = send(fin, rfin, sibling)
    last_swap.wait_recv()
    mine, other = fin[...], rfin[...]
    first = core == 0
    head = iota((16, C), 1) < 64
    for out, value in ((down_out, jnp.where(first, mine, other)), (up_out, jnp.where(first, other, mine))):
        fs[...] = pltpu.roll(value, 64, 1)
        second_half = jnp.where(head, fs[13:29, :], fs[14:30, :])
        half = jnp.where(first, value[0:16], second_half)
        for r in range(13):
            out[0:1, r * C : (r + 1) * C] = half[r : r + 1, :]
        out[0:1, 13 * C : 13 * C + 64] = half[13:14, 0:64]

    out_next.wait_recv()
    out_prev.wait_recv()
    out_next.wait_send()
    out_prev.wait_send()
    for copy in started:
        copy.wait_send()


N_COPIES = 15 + 8 + 15 + 3 + 3 + 1 + 2 + 8 + 3 + 15 + 1


def whole_step(act, par, sta, gra, dw, uw, coarse, nown, ncell, land):
    vm = pltpu.VMEM
    fine_rows = HT * WT
    scratch = [
        vm((9 * C, CP), BF), vm((CP, 16 * C), BF), vm((fine_rows, C), F32), vm((fine_rows, C), F32),
        vm((18, 40, C), F32), vm((18, 40, C), F32), vm((18, 40, C), F32), vm((18, 40, C), F32),
        vm((M2, 9 * C), BF), vm((M2, 16 * C), BF),
        vm((M2, CP), BF), vm((H2 + 1, 40, CP), F32), vm((H2 + 2, 48, CP), F32), vm((2, M2, C), F32),
        vm((CP, 16 * C), F32), vm((2, 9 * C, C), F32), vm((2, ROWS, C), F32), vm((ROWS, C), F32),
        vm((448, C), F32), vm((NZ, PADP, C), F32), vm((PADP, C), F32),
        vm((fine_rows, C), BF), vm((fine_rows, C), BF),
        vm((NTY, CAP, 128), BF), vm((NTY, CAP, 128), BF), vm((NTY, CAP, C), BF), vm((NTY, CAP, C), BF),
        vm((4 * WT, C), F32), vm((WT, C), F32),
        vm((2, WT, C), BF), vm((WT, C), BF), vm((2, HT, C), BF), vm((HT, C), BF),
        vm((2, WT, C), BF), vm((WT, C), BF), vm((2, HT, C), BF), vm((HT, C), BF),
        vm((2, HT, C), BF), vm((HT, C), BF), vm((HT, C), BF), vm((HT, C), BF),
        vm((W2, CP), BF), vm((H2, CP), BF), vm((W2, CP), BF), vm((H2, CP), BF), vm((H2, CP), BF),
        vm((WT, C), BF), vm((HT, C), BF), vm((WT, C), BF), vm((HT, C), BF), vm((HT, C), BF),
        vm((W2, CP), BF), vm((W2, CP), BF), vm((H2, CP), BF), vm((H2, CP), BF),
        vm((W2, CP), BF), vm((W2, CP), BF), vm((H2, CP), BF), vm((H2, CP), BF),
        vm((H2, CP), BF), vm((H2, CP), BF), vm((H2, CP), BF), vm((H2, CP), BF),
        vm((ROWS, C), BF), vm((ROWS, C), BF), vm((NY, QUART, C), BF), vm((NY - 1, QUART, C), BF),
        vm((NZ, PADP, C), BF), vm((NZ - 1, PADP, C), BF), vm((PADP, C), F32), vm((PADP, C), F32),
        pltpu.SemaphoreType.DMA((N_COPIES,)), pltpu.SemaphoreType.DMA((N_COPIES,)),
    ]
    in_vmem = pl.BlockSpec(memory_space=pltpu.VMEM)
    return pl.pallas_call(
        kernel,
        out_shape=(
            jax.ShapeDtypeStruct((fine_rows, C), BF),
            jax.ShapeDtypeStruct((fine_rows, C), BF),
            jax.ShapeDtypeStruct((1, ROWS), F32),
            jax.ShapeDtypeStruct((1, ROWS), F32),
        ),
        in_specs=[in_vmem] * 10,
        out_specs=(
            pl.BlockSpec(memory_space=pl.ANY), pl.BlockSpec(memory_space=pl.ANY), in_vmem, in_vmem,
        ),
        scratch_shapes=scratch,
        compiler_params=pltpu.CompilerParams(
            collective_id=0, has_side_effects=True, vmem_limit_bytes=56 << 20
        ),
        name="relay",
    )(act, par, sta, gra, dw, uw, coarse, nown, ncell, land)


def local(
    act_in, partner_in, stashed, grad_in, down_weights, up_weights, coarse, nest_owner, nest_cell,
    land_weight,
):
    flat = (HT * WT, C)
    from_before, from_after, down_sum, up_sum = whole_step(
        act_in.reshape(flat), partner_in.reshape(flat), stashed.reshape(flat), grad_in.reshape(flat),
        down_weights.reshape(9 * C, C2), up_weights.reshape(9, C2, C), coarse, nest_owner,
        nest_cell.reshape(1, CELLS), land_weight,
    )
    position = lax.axis_index("segment")
    zero = jnp.zeros((), BF)
    act_out = jnp.where(position == 0, zero, from_before)
    grad_out = jnp.where(position == NSEG - 1, zero, from_after)
    partner_out = jnp.where(position % 2 == 0, from_before, from_after)
    tile = (1, HT, WT, C)
    return (
        act_out.reshape(tile), grad_out.reshape(tile), partner_out.reshape(tile), down_sum, up_sum,
    )


def solution(mesh):
    placed = (
        P("segment", "tx", "ty", None),
        P("segment", "tx", "ty", None),
        P("segment", "tx", "ty", None),
        P("segment", "tx", "ty", None),
        P("segment", None, None, None, None),
        P("segment", None, None, None, None),
        P(("tx", "ty"), None),
        P(("tx", "ty"), None),
        P(("tx", "ty")),
        P("tx", "ty"),
    )
    return jax.shard_map(
        local,
        mesh=mesh,
        in_specs=placed,
        out_specs=(
            P("segment", "tx", "ty", None),
            P("segment", "tx", "ty", None),
            P("segment", "tx", "ty", None),
            P("segment", ("tx", "ty")),
            P("segment", ("tx", "ty")),
        ),
        check_vma=False,
    )
```

time: 564 us -> 74 us (0.13)
  waiting for transfers between devices: 341 us -> 0 us
  starting transfers between devices: 145 us -> 0 us
  Pallas kernels: 0 us -> 65.7 us
  local copies, waits for them, and re-layouts: 39 us -> 5.42 us
  between operations: 18 us -> 0.67 us
  other arithmetic: 10.9 us -> 1.93 us
  matrix products: 8.71 us -> 0 us
    unnamed x2 -> x0, waiting for transfers between devices: 327 us -> none
    ppermute x27 -> x0, starting transfers between devices: 121 us -> none  [the longest x11 91.4 us: padded_2(): before = lax.ppermute(last, axis, up)]
    pallas_call x0 -> x1, Pallas kernels: none -> 65.7 us  [whole_step(): pl.pallas_call(kernel, out_shape=(jax.ShapeDtypeStruct((fine_rows, C), BF...]
    all_to_all x2 -> x0, starting transfers between devices: 24.1 us -> none  [the longest x1 14 us: fetch_condition(): lax.all_to_all(request, 'ty', split_axis=0, concat_axis=0, tiled=True)]
    slice x16 -> x0, local copies, waits for them, and re-layouts: 14.9 us -> none  [the longest x9 13.4 us: kernel_grad(): padded[row_tap:row_tap + stride * (height - 1) + 1:stride, col_tap:col_ta...]
    ppermute x27 -> x0, waiting for transfers between devices: 10.6 us -> none  [the longest x12 10.6 us: padded_2(): after = lax.ppermute(leading, axis, down)]
    scatter x1 -> x0, local copies, waits for them, and re-layouts: 5.74 us -> none  [fetch_condition(): jnp.zeros((owners, capacity), jnp.int32).at[owner_ids, slot_ids]]
  transfers between devices with their start and end apart: 30 -> 0, of which waited for: 5 -> 0; matrix products, arithmetic and copies ran while one was open for 8% -> 0% of each run, Pallas kernels for 0% -> 0%
where the time goes in v1:
time: 74 us; the launch traced here: 73.7 us
  Pallas kernels  65.7 us (89%)
  local copies, waits for them, and re-layouts  5.42 us (7%)
  other arithmetic  1.93 us (3%)
    pallas_call x1, Pallas kernels, whole_step(): pl.pallas_call(kernel, out_shape=(jax.ShapeDtypeStruct((fine_rows, C), BF...  65.7 us
    unnamed x10, local copies, waits for them, and re-layouts  5.42 us
    select_n x1, other arithmetic, local(): partner_out = jnp.where(position % 2 == 0, from_before, from_after)  1.93 us

profile of v1, /device:TPU:1, one launch (start us, length us, event | category | flops | bytes accessed | tf_op | source)
XLA Modules:
  0.0 73.7 jit_solution(13989260924511991828)
XLA Ops:
  0.6 0.0 copy-start.2
  0.7 0.6 copy-done.2
  1.3 0.7 copy.16.nown
  2.0 2.1 %copy.15 = bf16[1,3,3,128,192]{4,3,2,1,0:T(8,128)(2,1)} copy(bf16[1,3,3,128,192]{3,4,2,1,0:T(8,128)(2,1)} %param.14) | data formatting | bytes 884736 | tf_op args[4]
  4.1 65.7 %relay.1 = (bf16[1024,128]{1,0:T(8,128)(2,1)}, bf16[1024,128]{1,0:T(8,128)(2,1)}, f32[1,1728]{1,0:T(1,128)}, f32[1,1728]{1,0:T(1,128)}) custom-call(bf16[1024,128]{1,0:T(8,128)(2,1)} %bitcast.15, bf16[1024,128]{1,0:T(8,128)(2,1)} %bitcast.16, bf16[1024,128]{1,0:T(8,128)(2,1)} %bitcast.17, bf16[1024,128]{1,0:T(8,128)(2,1)} %bitcast.18, ...), custom_call_target="tpu_custom_call" | custom-call | tf_op jit(solution)/shard_map/relay/pallas_call | solution.py:496
  69.8 1.9 %broadcast_select_fusion = (bf16[1024,128]{1,0:T(8,128)(2,1)}, bf16[1024,128]{1,0:T(8,128)(2,1)}, bf16[1024,128]{1,0:T(8,128)(2,1)}) fusion(bf16[1024,128]{1,0:T(8,128)(2,1)} %get-tuple-element.9, bf16[1024,128]{1,0:T(8,128)(2,1)} %get-tuple-element.10, pred[]{:T(512)S(6)} %eq.13, pred[]{:T(512)S(6)} %eq.12, pred[]{:T(512)S(6)} %eq.11), kind=kLoop, calls=%fused_computation | loop fusion | flops 393216 | bytes 1310723 | tf_op jit(solution)/shard_map/jit(_where)/select_n | solution.py:530
  71.7 0.0 copy-start.1
  71.7 0.7 copy-done.1
  72.4 0.0 copy-start
  72.4 0.6 copy.19
  73.0 0.1 copy-done
  73.1 0.6 copy.20
Async XLA Ops:
  0.6 0.7 copy-start.2
  71.7 0.7 copy-start.1
  72.4 0.7 copy-start

commit v2 on v1

--- a/solution.py
+++ b/solution.py
@@ -38,21 +38,32 @@
 
 
 def kernel(
+    act_h, par_h, sta_h, gra_h, dw_h, uw_h, coarse_h, nown_h, ncell_h, land_h,
+    left_out, right_out, down_out, up_out,
     act, par, sta, gra, dw, uw, coarse, nown, ncell, land,
-    left_out, right_out, down_out, up_out,
-    dwp, uc, t32, g32, soo, see, goo, gee, dim, wim,
+    dwp, uc, t32, g32, b32, soo, see, goo, gee, boo, bee, dim, dimf, dimg, wim,
     prb, pgf, rpf, r32, pw, gds, gf, gs, zs, zp, fs,
     pay_ig, pay_out,
     rqs, rqr, rps, rpr, condb, tr,
     srow_s, ogup_s, colr_s, coll_s,
     top_r, bot_r, lft_r, rgt_r, ctl_r, ctr_r, cbl_r, cbr_r,
     pgrow_s, pgcol_s, pgrow_r, pgcol_r, pgcor_r,
-    birow_s, bicol_s, birow_r, bicol_r, bicor_r,
-    rdt_s, rdb_s, rdl_s, rdr_s,
-    rdt_r, rdb_r, rdl_r, rdr_r, rtl_r, rtr_r, rbl_r, rbr_r,
+    birow_s, biup_s, bicol_s, birow_r, biup_r, bicol_r, bicor_r, bibl_r,
+    rdb_s, rdl_s, rdr_s, rel_s, rer_s,
+    rdt_r, rdl_r, rdr_r, rtl_r, rtr_r, rel_r, rer_r,
     gb, ra, yb, ry, zb, rz, fin, rfin,
-    ssem, rsem,
+    ssem, rsem, isem,
 ):
+    bring = [
+        pltpu.make_async_copy(src, dst, isem.at[i])
+        for i, (src, dst) in enumerate((
+            (nown_h, nown), (ncell_h, ncell), (land_h, land), (gra_h, gra), (par_h, par), (sta_h, sta),
+            (coarse_h, coarse), (act_h, act), (uw_h, uw), (dw_h, dw),
+        ))
+    ]
+    for copy in bring:
+        copy.start()
+
     seg, tx, ty = lax.axis_index("segment"), lax.axis_index("tx"), lax.axis_index("ty")
     core = lax.rem(ty, 2)
     zl = ty // 2
@@ -106,22 +117,29 @@
         started.append(copy)
         return copy
 
+    def arrived(name, copies):
+        with jax.named_scope("await_" + name):
+            for copy in copies:
+                copy.wait_recv()
+
     not_top, not_bottom = tx > 0, tx < NTX - 1
     not_left, not_right = ty > 0, ty < NTY - 1
 
     def keep(flag, value):
         return jnp.where(flag, value, 0.0)
 
+    for copy in bring[:3]:
+        copy.wait()
     decoder = (seg >= NSEG // 2).astype(F32)
     encoder = 1.0 - decoder
 
     def iota(shape, axis):
         return lax.broadcasted_iota(jnp.int32, shape, axis)
 
-    ocol = nown[...].astype(F32)
+    orow = nown[...].astype(F32)
     crow = ncell[...].astype(F32)
     n0, n1 = iota((CELLS, CELLS), 0), iota((CELLS, CELLS), 1)
-    orow = jnp.sum(jnp.where(n0 == n1, ocol, 0.0), axis=0, keepdims=True)
+    ocol = jnp.sum(jnp.where(n0 == n1, orow, 0.0), axis=1, keepdims=True)
     ccol = jnp.sum(jnp.where(n0 == n1, crow, 0.0), axis=1, keepdims=True)
     same = jnp.where(ocol == orow, 1.0, 0.0)
     slot_row = jnp.sum(jnp.where(n0 < n1, same, 0.0), axis=0, keepdims=True)
@@ -140,6 +158,8 @@
         rqs[q] = asked[q * CAP : (q + 1) * CAP].astype(BF)
     rqr[0] = rqs[0]
 
+    for copy in bring[3:6]:
+        copy.wait()
     spread = iota((WT, WT // 4), 1) == (iota((WT, WT // 4), 0) >> 2)
     for k in range(HT // 4):
         row = land[k : k + 1, :].astype(F32)
@@ -159,7 +179,8 @@
     colr_s[1] = g32[pl.ds(WT - 1, HT, stride=WT), :].astype(BF)
     coll_s[...] = g32[pl.ds(0, HT, stride=WT), :].astype(BF)
 
-    pl.semaphore_wait(barrier, len(greeted))
+    with jax.named_scope("await_entry"):
+        pl.semaphore_wait(barrier, len(greeted))
 
     request = [send(rqs.at[q], rqr.at[q], ty_peer(q)) for q in range(1, NTY)]
     rim = [
@@ -173,8 +194,11 @@
         send(coll_s, rgt_r, at(0, -1)),
     ]
 
-    dwp[:, 0:C2] = dw[...]
-    dwp[:, C2:CP] = jnp.zeros((9 * C, CP - C2), BF)
+    for copy in bring[6:]:
+        copy.wait()
+    dwp[C2:CP, :] = jnp.zeros((CP - C2, 9 * C), BF)
+    for t in range(9):
+        dwp[0:C2, t * C : (t + 1) * C] = dw[t]
     uc[C2:CP, :] = jnp.zeros((CP - C2, 16 * C), BF)
     for u in range(4):
         for v in range(4):
@@ -212,19 +236,19 @@
         halves = [r32[h, pl.ds(j, H2, stride=W2), :] for h in range(2)]
         return jnp.concatenate(halves, axis=1).astype(BF)
 
-    def gather_down(oo, ee):
-        views = [oo[:, 7:39, :], ee[:, 0:32, :], oo[:, 8:40, :]]
-        for b, view in enumerate(views):
-            view = view.astype(BF)
+    def gather_down(oo, ee, first, n, lhs, row):
+        span = slice(2 * first, 2 * first + 2 * n + 2)
+        for b, view in enumerate([oo[span, 7:39, :], ee[span, 0:32, :], oo[span, 8:40, :]]):
+            pairs = view.astype(BF).reshape(n + 1, 2, W2, C)
             for a in range(3):
                 block = (a * 3 + b) * C
-                dim[:, block : block + C] = rows_of(view, a)
+                part = pairs[a // 2 : a // 2 + n, a % 2].reshape(n * W2, C)
+                lhs[row : row + n * W2, block : block + C] = part
 
     fill(soo, see, t32)
     fill(goo, gee, g32)
 
-    for copy in request:
-        copy.wait_recv()
+    arrived("request", request)
     wanted = jnp.concatenate([rqr[q].astype(F32) for q in range(NTY)], axis=0)
     answer = dot(wanted[:, 0:CELLS].astype(BF), coarse[...])
     for q in range(NTY):
@@ -234,8 +258,7 @@
         send(rps.at[q], rpr.at[q], (seg, tx, lax.rem(ty + NTY - q, NTY))) for q in range(1, NTY)
     ]
 
-    for copy in rim:
-        copy.wait_recv()
+    arrived("rim", rim)
     fill_row(soo, see, 0, not_top, top_r[0])
     fill_row(goo, gee, 0, not_top, top_r[1])
     fill_row(goo, gee, 17, not_bottom, bot_r[...])
@@ -248,14 +271,14 @@
     fill_cell(goo, 17, 7, not_bottom & not_left, cbl_r[...], 0)
     fill_cell(gee, 17, W2, not_bottom & not_right, cbr_r[...], 0)
 
-    gather_down(soo, see)
+    gather_down(soo, see, 0, H2, dim, 0)
     for v, view in enumerate([goo[:, 7:39, :], gee[:, 0:32, :], goo[:, 8:40, :], gee[:, 1:33, :]]):
         view = view.astype(BF)
         for u in range(4):
             block = (u * 4 + v) * C
             wim[:, block : block + C] = rows_of(view, u)
 
-    pre_back = dot(dim[...], dwp[...])
+    pre_back = dot(dim[...], dwp[...], ((1,), (1,)))
     gate = jax.nn.sigmoid(pre_back)
     prb[...] = (pre_back * gate).astype(BF)
     pooled = dot(wim[...], uc[...], ((1,), (1,)))
@@ -270,31 +293,6 @@
         send(pgcol_s, pgcol_r, at(0, -1)),
     ]
     pgf[0:H2, 0:W2, :] = half_grid.reshape(H2, W2, CP)
-
-    for copy in reply:
-        copy.wait_recv()
-    table = jnp.concatenate([rpr[q].astype(F32) for q in range(NTY)], axis=0).astype(BF)
-    pick = jnp.where(iota((CELLS, NTY * CAP), 1).astype(F32) == qcol, 1.0, 0.0).astype(BF)
-    fetched = dot(pick, table).astype(BF)
-    r0, r1 = iota((4 * WT, CELLS), 0), iota((4 * WT, CELLS), 1)
-    widen = jnp.where(r1 == ((r0 >> 6) << 4) + ((r0 & 63) >> 2), 1.0, 0.0).astype(BF)
-    condb[...] = dot(widen, fetched)
-    for y in range(HT):
-        part = pl.ds(y * WT, WT)
-        value = (
-            act[part, :].astype(F32)
-            + decoder * par[part, :].astype(F32)
-            + condb[pl.ds(y // 4 * WT, WT), :]
-        )
-        t32[part, :] = value.astype(BF).astype(F32)
-    birow_s[...] = t32[last : last + WT, :].astype(BF)
-    bicol_s[...] = t32[pl.ds(WT - 1, HT, stride=WT), :].astype(BF)
-    bi_rim = [
-        send(birow_s, birow_r, at(1, 0)),
-        send(bicol_s, bicor_r, at(1, 1)),
-        send(bicol_s, bicol_r, at(0, 1)),
-    ]
-    fill(soo, see, t32)
 
     product = dot(dim[...], pre_grad, ((0,), (0,)))
     gds[0] = product[:, 0:C]
@@ -321,8 +319,39 @@
     gb[...] = gf[1 - core].astype(BF)
     swap = send(gb, ra, sibling)
 
-    for copy in pg_rim:
-        copy.wait_recv()
+    arrived("swap", [swap])
+    gs[...] = gf[core] + ra[...].astype(F32)
+    yb[...] = gs[...].astype(BF).reshape(NY, QUART, C)
+    y_sum = [send(yb.at[lax.rem(yy + q, NY)], ry.at[q - 1], y_peer(q)) for q in range(1, NY)]
+
+    arrived("reply", reply)
+    table = jnp.concatenate([rpr[q].astype(F32) for q in range(NTY)], axis=0).astype(BF)
+    pick = jnp.where(iota((CELLS, NTY * CAP), 1).astype(F32) == qcol, 1.0, 0.0).astype(BF)
+    fetched = dot(pick, table).astype(BF)
+    r0, r1 = iota((4 * WT, CELLS), 0), iota((4 * WT, CELLS), 1)
+    widen = jnp.where(r1 == ((r0 >> 6) << 4) + ((r0 & 63) >> 2), 1.0, 0.0).astype(BF)
+    condb[...] = dot(widen, fetched)
+    for y in range(HT):
+        part = pl.ds(y * WT, WT)
+        value = (
+            act[part, :].astype(F32)
+            + decoder * par[part, :].astype(F32)
+            + condb[pl.ds(y // 4 * WT, WT), :]
+        )
+        b32[part, :] = value.astype(BF).astype(F32)
+    birow_s[...] = b32[last : last + WT, :].astype(BF)
+    bicol_s[...] = b32[pl.ds(WT - 1, HT, stride=WT), :].astype(BF)
+    biup_s[...] = b32[0 : 2 * WT, :].astype(BF)
+    bi_tx = [
+        send(birow_s, birow_r, at(1, 0)),
+        send(biup_s, biup_r, at(-1, 0)),
+        send(bicol_s, bicor_r, at(1, 1)),
+        send(bicol_s, bibl_r, at(-1, 1)),
+    ]
+    bi_ty = [send(bicol_s, bicol_r, at(0, 1))]
+    fill(boo, bee, b32)
+
+    arrived("pg_rim", pg_rim)
     pgf[H2, 0:W2, :] = keep(not_bottom, pgrow_r[...].astype(F32))
     fill_col(pgf, 0, W2, not_right, pgcol_r[...])
     fill_cell(pgf, H2, W2, not_bottom & not_right, pgcor_r[...], 0)
@@ -342,91 +371,66 @@
             for a, di in ((1, 0),) if pr == 0 else ((2, 0), (0, 1)):
                 for b, dj in ((1, 0),) if pc == 0 else ((2, 0), (0, 1)):
                     tap = (a * 3 + b) * C
-                    value = value + dot(shifted[di][dj], dwp[tap : tap + C, :], ((1,), (1,)))
+                    value = value + dot(shifted[di][dj], dwp[:, tap : tap + C])
             spread_out(value, pr, pc)
     pay_ig[...] = t32[...].astype(BF)
 
-    up_slot, down_slot = slot(), slot()
-    ig_next = make(up_slot, pay_ig, left_out, seg_next)
-    ig_prev = make(down_slot, pay_ig, right_out, seg_prev)
-    out_next = make(up_slot, pay_out, left_out, seg_next)
-    out_prev = make(down_slot, pay_out, right_out, seg_prev)
+    parts = [pl.ds(3 * WT, 12 * WT), pl.ds(0, 3 * WT), pl.ds(15 * WT, WT)]
+    slots = [(slot(), slot()) for _ in parts]
+
+    def block_copies(source):
+        return [
+            (make(up, source.at[part, :], left_out.at[part, :], seg_next),
+             make(down, source.at[part, :], right_out.at[part, :], seg_prev))
+            for part, (up, down) in zip(parts, slots)
+        ]
+
+    ig_copies, out_copies = block_copies(pay_ig), block_copies(pay_out)
 
     @pl.when(seg == NSEG - 1)
     def _():
-        ig_next.start()
+        for copy, _ in ig_copies:
+            copy.start()
 
     @pl.when(seg >= 1)
     def _():
-        ig_prev.start()
-
-    for copy in bi_rim:
-        copy.wait_recv()
-    fill_row(soo, see, 0, not_top, birow_r[...])
-    fill_col(soo, 1, 7, not_left, bicol_r[...])
-    fill_cell(soo, 0, 7, not_top & not_left, bicor_r[...], HT - 1)
-    gather_down(soo, see)
-    pre_down = dot(dim[...], dwp[...])
-    half_grid = (pre_down * jax.nn.sigmoid(pre_down)).astype(BF).astype(F32)
-    put_half(half_grid)
-    rdt_s[...] = half_grid[0:W2].astype(BF)
-    rdb_s[...] = half_grid[M2 - W2 : M2].astype(BF)
+        for _, copy in ig_copies:
+            copy.start()
+
+    def send_output(which):
+        @pl.when(seg <= NSEG - 2)
+        def _():
+            for k in which:
+                out_copies[k][0].start()
+
+        @pl.when(seg == 0)
+        def _():
+            for k in which:
+                out_copies[k][1].start()
+
+    def reduce(lhs):
+        pre_down = dot(lhs[...], dwp[...], ((1,), (1,)))
+        return (pre_down * jax.nn.sigmoid(pre_down)).astype(BF).astype(F32)
+
+    arrived("bi_ty", bi_ty)
+    fill_col(boo, 1, 7, not_left, bicol_r[...])
+    gather_down(boo, bee, 1, H2 - 1, dimf, 0)
+    half_grid = reduce(dimf)
+    r32[0, W2:M2, :] = half_grid[:, 0:C]
+    r32[1, W2:M2, :] = half_grid[:, C:CP]
+    rdb_s[...] = half_grid[M2 - 2 * W2 :].astype(BF)
     rdl_s[...] = half_col(0)
     rdr_s[...] = half_col(W2 - 1)
     red_rim = [
         send(rdb_s, rdt_r, at(1, 0)),
-        send(rdt_s, rdb_r, at(-1, 0)),
         send(rdr_s, rtl_r, at(1, 1)),
         send(rdl_s, rtr_r, at(1, -1)),
-        send(rdr_s, rbl_r, at(-1, 1)),
-        send(rdl_s, rbr_r, at(-1, -1)),
         send(rdr_s, rdl_r, at(0, 1)),
         send(rdl_s, rdr_r, at(0, -1)),
     ]
-    rpf[1 : H2 + 1, 8:40, :] = half_grid.reshape(H2, W2, CP)
-
-    swap.wait_recv()
-    gs[...] = gf[core] + ra[...].astype(F32)
-    yb[...] = gs[...].astype(BF).reshape(NY, QUART, C)
-    y_sum = [send(yb.at[lax.rem(yy + q, NY)], ry.at[q - 1], y_peer(q)) for q in range(1, NY)]
-
-    for copy in red_rim:
-        copy.wait_recv()
-    rpf[0, 8:40, :] = keep(not_top, rdt_r[...].astype(F32))
-    rpf[H2 + 1, 8:40, :] = keep(not_bottom, rdb_r[...].astype(F32))
-    fill_col(rpf, 1, 7, not_left, rdl_r[...])
-    fill_col(rpf, 1, 40, not_right, rdr_r[...])
-    fill_cell(rpf, 0, 7, not_top & not_left, rtl_r[...], H2 - 1)
-    fill_cell(rpf, 0, 40, not_top & not_right, rtr_r[...], H2 - 1)
-    fill_cell(rpf, H2 + 1, 7, not_bottom & not_left, rbl_r[...], 0)
-    fill_cell(rpf, H2 + 1, 40, not_bottom & not_right, rbr_r[...], 0)
-    moved = {}
-    for dj in range(3):
-        view = rpf[:, 7 + dj : 39 + dj, :].astype(BF)
-        for di in range(3):
-            moved[di, dj] = view[di : di + H2].reshape(M2, CP)
-    meets = (((0, 3), (1, 1)), ((1, 2), (2, 0)))
-    for pr in range(2):
-        for pc in range(2):
-            plane = see[:, 0:32, :] if pc == 0 else soo[:, 8:40, :]
-            value = rows_of(plane, 1 + pr)
-            for di, u in meets[pr]:
-                for dj, v in meets[pc]:
-                    block = (u * 4 + v) * C
-                    value = value + dot(moved[di, dj], uc[:, block : block + C])
-            spread_out(value, pr, pc)
-    pay_out[...] = t32[...].astype(BF)
-
-    @pl.when(seg <= NSEG - 2)
-    def _():
-        out_next.start()
-
-    @pl.when(seg == 0)
-    def _():
-        out_prev.start()
-
-    for copy in y_sum:
-        copy.wait_recv()
+    rpf[2 : H2 + 1, 8:40, :] = half_grid.reshape(H2 - 1, W2, CP)
+
+    arrived("y_sum", y_sum)
     total = gs[pl.ds(yy * QUART, QUART), :]
     for q in range(NY - 1):
         total = total + ry[q].astype(F32)
@@ -436,15 +440,68 @@
         zp[z] = zs[z * PIECE : z * PIECE + PADP, :]
     zb[...] = zp[...].astype(BF)
     z_sum = [send(zb.at[lax.rem(zz + q, NZ)], rz.at[q - 1], z_peer(q)) for q in range(1, NZ)]
-    for copy in z_sum:
-        copy.wait_recv()
+    arrived("bi_tx", bi_tx)
+    fill_row(boo, bee, 0, not_top, birow_r[...])
+    fill_cell(boo, 0, 7, not_top & not_left, bicor_r[...], HT - 1)
+    for k in range(2):
+        fill_row(boo, bee, 17 + k, not_bottom, biup_r[k * WT : (k + 1) * WT, :])
+        fill_cell(boo, 17 + k, 7, not_bottom & not_left, bibl_r[...], k)
+    gather_down(boo, bee, 0, 1, dimg, 0)
+    gather_down(boo, bee, H2, 1, dimg, W2)
+    half_grid = reduce(dimg)
+    upper = iota((8, CP), 0) == 0
+    rel_s[...] = jnp.where(upper, half_grid[0:1], half_grid[W2 : W2 + 1]).astype(BF)
+    rer_s[...] = jnp.where(upper, half_grid[W2 - 1 : W2], half_grid[2 * W2 - 1 :]).astype(BF)
+    red_late = [send(rer_s, rel_r, at(0, 1)), send(rel_s, rer_r, at(0, -1))]
+    rpf[1, 8:40, :] = half_grid[0:W2]
+    rpf[H2 + 1, 8:40, :] = keep(not_bottom, half_grid[W2:])
+
+    arrived("red_rim", red_rim)
+    rpf[0, 8:40, :] = keep(not_top, rdt_r[...].astype(F32))
+    fill_col(rpf, 1, 7, not_left, rdl_r[...])
+    fill_col(rpf, 1, 40, not_right, rdr_r[...])
+    fill_cell(rpf, 0, 7, not_top & not_left, rtl_r[...], H2 - 1)
+    fill_cell(rpf, 0, 40, not_top & not_right, rtr_r[...], H2 - 1)
+    meets = (((0, 3), (1, 1)), ((1, 2), (2, 0)))
+
+    def output_rows(pr, first, n):
+        for pc in range(2):
+            span = slice(2 * first + pr + 1, 2 * first + pr + 1 + 2 * n)
+            plane = bee[span, 0:32, :] if pc == 0 else boo[span, 8:40, :]
+            value = plane.reshape(n, 2, W2, C)[:, 0].reshape(n * W2, C)
+            for di, u in meets[pr]:
+                for dj, v in meets[pc]:
+                    block = (u * 4 + v) * C
+                    lhs = rpf[first + di : first + di + n, 7 + dj : 39 + dj, :]
+                    lhs = lhs.astype(BF).reshape(n * W2, CP)
+                    value = value + dot(lhs, uc[:, block : block + C])
+            for k in range(n):
+                start = (2 * (first + k) + pr) * WT + pc
+                t32[pl.ds(start, W2, stride=2), :] = value[k * W2 : (k + 1) * W2]
+
+    output_rows(0, 2, 6)
+    output_rows(1, 1, 6)
+    pay_out[3 * WT : 15 * WT, :] = t32[3 * WT : 15 * WT, :].astype(BF)
+    send_output((0,))
+    arrived("red_late", red_late)
+    for column, flag, got in ((7, not_left, rel_r), (40, not_right, rer_r)):
+        fill_cell(rpf, 1, column, flag, got[...], 0)
+        fill_cell(rpf, H2 + 1, column, flag & not_bottom, got[...], 1)
+    output_rows(0, 0, 2)
+    output_rows(1, 0, 1)
+    output_rows(1, H2 - 1, 1)
+    pay_out[0 : 3 * WT, :] = t32[0 : 3 * WT, :].astype(BF)
+    pay_out[15 * WT :, :] = t32[15 * WT :, :].astype(BF)
+    send_output((1, 2))
+
+    arrived("z_sum", z_sum)
     total = zp[zz]
     for q in range(NZ - 1):
         total = total + rz[q].astype(F32)
     scaling = 1.0 / math.sqrt(HT * WT * NTX * NTY)
     fin[...] = total * scaling
     last_swap = send(fin, rfin, sibling)
-    last_swap.wait_recv()
+    arrived("last_swap", [last_swap])
     mine, other = fin[...], rfin[...]
     first = core == 0
     head = iota((16, C), 1) < 64
@@ -456,24 +513,88 @@
             out[0:1, r * C : (r + 1) * C] = half[r : r + 1, :]
         out[0:1, 13 * C : 13 * C + 64] = half[13:14, 0:64]
 
-    out_next.wait_recv()
-    out_prev.wait_recv()
-    out_next.wait_send()
-    out_prev.wait_send()
+    with jax.named_scope("await_blocks"):
+        for pair in out_copies:
+            for copy in pair:
+                copy.wait_recv()
+    for pair in out_copies:
+        for copy in pair:
+            copy.wait_send()
     for copy in started:
         copy.wait_send()
 
 
-N_COPIES = 15 + 8 + 15 + 3 + 3 + 1 + 2 + 8 + 3 + 15 + 1
+def finish(left_h, right_h, down_h, up_h, act_o, grad_o, partner_o, down_o, up_o,
+           left, right, down, up, blank, isem, osem):
+    seg = lax.axis_index("segment")
+    even = lax.rem(seg, 2) == 0
+    bring = [
+        pltpu.make_async_copy(src, dst, isem.at[i])
+        for i, (src, dst) in enumerate(((left_h, left), (right_h, right), (down_h, down), (up_h, up)))
+    ]
+    for copy in bring:
+        copy.start()
+
+    @pl.when((seg == 0) | (seg == NSEG - 1))
+    def _():
+        blank[...] = jnp.zeros_like(blank)
+
+    ends = [
+        pltpu.make_async_copy(left, act_o, osem.at[0]),
+        pltpu.make_async_copy(right, grad_o, osem.at[1]),
+        pltpu.make_async_copy(left, partner_o, osem.at[2]),
+        pltpu.make_async_copy(down, down_o, osem.at[3]),
+        pltpu.make_async_copy(up, up_o, osem.at[4]),
+    ]
+
+    @pl.when(seg == 0)
+    def _():
+        pltpu.make_async_copy(blank, act_o, osem.at[0]).start()
+
+    @pl.when(seg == NSEG - 1)
+    def _():
+        pltpu.make_async_copy(blank, grad_o, osem.at[1]).start()
+
+    for copy in bring:
+        copy.wait()
+
+    @pl.when(seg > 0)
+    def _():
+        ends[0].start()
+
+    @pl.when(seg < NSEG - 1)
+    def _():
+        ends[1].start()
+
+    @pl.when(even)
+    def _():
+        ends[2].start()
+
+    @pl.when(jnp.logical_not(even))
+    def _():
+        pltpu.make_async_copy(right, partner_o, osem.at[2]).start()
+
+    ends[3].start()
+    ends[4].start()
+    for copy in ends:
+        copy.wait()
+
+
+N_COPIES = 15 + 8 + 15 + 3 + 1 + 3 + 5 + 6 + 5 + 15 + 2 + 1
 
 
 def whole_step(act, par, sta, gra, dw, uw, coarse, nown, ncell, land):
     vm = pltpu.VMEM
     fine_rows = HT * WT
     scratch = [
-        vm((9 * C, CP), BF), vm((CP, 16 * C), BF), vm((fine_rows, C), F32), vm((fine_rows, C), F32),
+        vm((fine_rows, C), BF), vm((fine_rows, C), BF), vm((fine_rows, C), BF), vm((fine_rows, C), BF),
+        vm((9, C2, C), BF), vm((9, C2, C), BF), vm((CELLS, C), BF), vm((1, CELLS), jnp.int32),
+        vm((1, CELLS), jnp.int32), vm((HT // 4, WT // 4), jnp.int32),
+        vm((CP, 9 * C), BF), vm((CP, 16 * C), BF), vm((fine_rows, C), F32), vm((fine_rows, C), F32),
+        vm((fine_rows, C), F32),
         vm((18, 40, C), F32), vm((18, 40, C), F32), vm((18, 40, C), F32), vm((18, 40, C), F32),
-        vm((M2, 9 * C), BF), vm((M2, 16 * C), BF),
+        vm((20, 40, C), F32), vm((20, 40, C), F32),
+        vm((M2, 9 * C), BF), vm((M2 - W2, 9 * C), BF), vm((2 * W2, 9 * C), BF), vm((M2, 16 * C), BF),
         vm((M2, CP), BF), vm((H2 + 1, 40, CP), F32), vm((H2 + 2, 48, CP), F32), vm((2, M2, C), F32),
         vm((CP, 16 * C), F32), vm((2, 9 * C, C), F32), vm((2, ROWS, C), F32), vm((ROWS, C), F32),
         vm((448, C), F32), vm((NZ, PADP, C), F32), vm((PADP, C), F32),
@@ -484,13 +605,15 @@
         vm((2, WT, C), BF), vm((WT, C), BF), vm((2, HT, C), BF), vm((HT, C), BF),
         vm((2, HT, C), BF), vm((HT, C), BF), vm((HT, C), BF), vm((HT, C), BF),
         vm((W2, CP), BF), vm((H2, CP), BF), vm((W2, CP), BF), vm((H2, CP), BF), vm((H2, CP), BF),
-        vm((WT, C), BF), vm((HT, C), BF), vm((WT, C), BF), vm((HT, C), BF), vm((HT, C), BF),
-        vm((W2, CP), BF), vm((W2, CP), BF), vm((H2, CP), BF), vm((H2, CP), BF),
-        vm((W2, CP), BF), vm((W2, CP), BF), vm((H2, CP), BF), vm((H2, CP), BF),
-        vm((H2, CP), BF), vm((H2, CP), BF), vm((H2, CP), BF), vm((H2, CP), BF),
+        vm((WT, C), BF), vm((2 * WT, C), BF), vm((HT, C), BF),
+        vm((WT, C), BF), vm((2 * WT, C), BF), vm((HT, C), BF), vm((HT, C), BF), vm((HT, C), BF),
+        vm((W2, CP), BF), vm((H2, CP), BF), vm((H2, CP), BF), vm((8, CP), BF), vm((8, CP), BF),
+        vm((W2, CP), BF), vm((H2, CP), BF), vm((H2, CP), BF), vm((H2, CP), BF), vm((H2, CP), BF),
+        vm((8, CP), BF), vm((8, CP), BF),
         vm((ROWS, C), BF), vm((ROWS, C), BF), vm((NY, QUART, C), BF), vm((NY - 1, QUART, C), BF),
         vm((NZ, PADP, C), BF), vm((NZ - 1, PADP, C), BF), vm((PADP, C), F32), vm((PADP, C), F32),
         pltpu.SemaphoreType.DMA((N_COPIES,)), pltpu.SemaphoreType.DMA((N_COPIES,)),
+        pltpu.SemaphoreType.DMA((10,)),
     ]
     in_vmem = pl.BlockSpec(memory_space=pltpu.VMEM)
     return pl.pallas_call(
@@ -501,7 +624,7 @@
             jax.ShapeDtypeStruct((1, ROWS), F32),
             jax.ShapeDtypeStruct((1, ROWS), F32),
         ),
-        in_specs=[in_vmem] * 10,
+        in_specs=[pl.BlockSpec(memory_space=pl.ANY)] * 10,
         out_specs=(
             pl.BlockSpec(memory_space=pl.ANY), pl.BlockSpec(memory_space=pl.ANY), in_vmem, in_vmem,
         ),
@@ -520,14 +643,25 @@
     flat = (HT * WT, C)
     from_before, from_after, down_sum, up_sum = whole_step(
         act_in.reshape(flat), partner_in.reshape(flat), stashed.reshape(flat), grad_in.reshape(flat),
-        down_weights.reshape(9 * C, C2), up_weights.reshape(9, C2, C), coarse, nest_owner,
+        jnp.swapaxes(down_weights, 3, 4).reshape(9, C2, C), up_weights.reshape(9, C2, C), coarse,
+        nest_owner.reshape(1, CELLS),
         nest_cell.reshape(1, CELLS), land_weight,
     )
-    position = lax.axis_index("segment")
-    zero = jnp.zeros((), BF)
-    act_out = jnp.where(position == 0, zero, from_before)
-    grad_out = jnp.where(position == NSEG - 1, zero, from_after)
-    partner_out = jnp.where(position % 2 == 0, from_before, from_after)
+    block = jax.ShapeDtypeStruct(flat, BF)
+    sums = jax.ShapeDtypeStruct((1, ROWS), F32)
+    anywhere = pl.BlockSpec(memory_space=pl.ANY)
+    act_out, grad_out, partner_out, down_sum, up_sum = pl.pallas_call(
+        finish,
+        out_shape=(block, block, block, sums, sums),
+        in_specs=[anywhere] * 4,
+        out_specs=(anywhere,) * 5,
+        scratch_shapes=[
+            pltpu.VMEM(flat, BF), pltpu.VMEM(flat, BF), pltpu.VMEM((1, ROWS), F32),
+            pltpu.VMEM((1, ROWS), F32), pltpu.VMEM(flat, BF),
+            pltpu.SemaphoreType.DMA((4,)), pltpu.SemaphoreType.DMA((5,)),
+        ],
+        name="finish",
+    )(from_before, from_after, down_sum, up_sum)
     tile = (1, HT, WT, C)
     return (
         act_out.reshape(tile), grad_out.reshape(tile), partner_out.reshape(tile), down_sum, up_sum,

time: 74 us -> 62.9 us (0.85)
  the two profiles are of different devices: /device:TPU:1 before, /device:TPU:102 now
where the time goes in v2:
time: 62.9 us; the launch traced here: 62.7 us
  Pallas kernels  62.1 us (99%)
  between operations  0.64 us (1%)
    pallas_call x1, Pallas kernels, whole_step(): pl.pallas_call(kernel, out_shape=(jax.ShapeDtypeStruct((fine_rows, C), BF...  60.1 us
    pallas_call x1, Pallas kernels, local(): pl.pallas_call(finish, out_shape=(block, block, block, sums, sums), in_sp...  2 us

profile of v2, /device:TPU:102, one launch (start us, length us, event | category | flops | bytes accessed | tf_op | source)
XLA Modules:
  0.0 62.7 jit_solution(3008612415714438005)
XLA Ops:
  0.6 60.1 %relay.1 = (bf16[1024,128]{1,0:T(8,128)(2,1)}, bf16[1024,128]{1,0:T(8,128)(2,1)}, f32[1,1728]{1,0:T(1,128)}, f32[1,1728]{1,0:T(1,128)}) custom-call(bf16[1024,128]{1,0:T(8,128)(2,1)} %bitcast.15, bf16[1024,128]{1,0:T(8,128)(2,1)} %bitcast.16, bf16[1024,128]{1,0:T(8,128)(2,1)} %bitcast.17, bf16[1024,128]{1,0:T(8,128)(2,1)} %bitcast.18, ...), custom_call_target="tpu_custom_call" | custom-call | tf_op jit(solution)/shard_map/relay/pallas_call | solution.py:619
  60.7 2.0 %finish.1 = (bf16[1024,128]{1,0:T(8,128)(2,1)}, bf16[1024,128]{1,0:T(8,128)(2,1)}, bf16[1024,128]{1,0:T(8,128)(2,1)}, f32[1,1728]{1,0:T(1,128)}, f32[1,1728]{1,0:T(1,128)}) custom-call(bf16[1024,128]{1,0:T(8,128)(2,1)} %get-tuple-element.14.left_h, bf16[1024,128]{1,0:T(8,128)(2,1)} %get-tuple-element.15.right_h, f32[1,1728]{1,0:T(1,128)} %get-tuple-element.16.down_h, ...), custom_call_target="tpu_custom_call" | custom-call | tf_op jit(solution)/shard_map/finish/pallas_call | solution.py:653

commit v3 on v2

--- a/solution.py
+++ b/solution.py
@@ -23,6 +23,7 @@
 QUART = ROWS // NY
 PIECE = QUART // NZ
 PADP = 32
+FAR_FIRST = (8, 7, 9, 6, 10, 5, 11, 4, 12, 3, 13, 2, 14, 1, 15)
 TAPS_OF = ((2,), (1, 2), (0, 1), (0,))
 
 
@@ -41,8 +42,8 @@
     act_h, par_h, sta_h, gra_h, dw_h, uw_h, coarse_h, nown_h, ncell_h, land_h,
     left_out, right_out, down_out, up_out,
     act, par, sta, gra, dw, uw, coarse, nown, ncell, land,
-    dwp, uc, t32, g32, b32, soo, see, goo, gee, boo, bee, dim, dimf, dimg, wim,
-    prb, pgf, rpf, r32, pw, gds, gf, gs, zs, zp, fs,
+    dwp, uc, t32, g32, b32, soo, see, goo, gee, boo, bee, dim, dimf, dimg, dimh, wim, wimg,
+    pgf, rpf, r32, pw, gds, gf, gs, zs, zp, fs,
     pay_ig, pay_out,
     rqs, rqr, rps, rpr, condb, tr,
     srow_s, ogup_s, colr_s, coll_s,
@@ -54,6 +55,40 @@
     gb, ra, yb, ry, zb, rz, fin, rfin,
     ssem, rsem, isem,
 ):
+    seg, tx, ty = lax.axis_index("segment"), lax.axis_index("tx"), lax.axis_index("ty")
+    core = lax.rem(ty, 2)
+    zl = ty // 2
+    zh = lax.rem(tx, 2)
+    yy = tx // 2
+    zz = zh * 8 + zl
+
+    def at(dx, dy):
+        return (seg, lax.rem(tx + dx + NTX, NTX), lax.rem(ty + dy + NTY, NTY))
+
+    def ty_peer(q):
+        return (seg, tx, lax.rem(ty + q, NTY))
+
+    def y_peer(q):
+        return (seg, lax.rem(yy + q, NY) * 2 + zh, ty)
+
+    def z_peer(q):
+        z = lax.rem(zz + q, NZ)
+        return (seg, yy * 2 + z // 8, lax.rem(z, 8) * 2 + core)
+
+    sibling = (seg, tx, zl * 2 + 1 - core)
+    seg_next = (lax.rem(seg + 1, NSEG), tx, ty)
+    seg_prev = (lax.rem(seg + NSEG - 1, NSEG), tx, ty)
+
+    barrier = pltpu.get_barrier_semaphore()
+    around = [(1, 0), (-1, 0), (0, 1), (0, -1), (1, 1), (1, -1), (-1, 1), (-1, -1)]
+    greeted = [at(dx, dy) for dx, dy in around if dx != 0]
+    greeted += [ty_peer(q) for q in range(1, NTY)]
+    greeted += [y_peer(q) for q in range(1, NY)]
+    greeted += [z_peer(q) for q in range(1, NZ)]
+    greeted += [seg_next, seg_prev]
+    for device in greeted:
+        pl.semaphore_signal(barrier, inc=1, device_id=device, device_id_type=MESH)
+
     bring = [
         pltpu.make_async_copy(src, dst, isem.at[i])
         for i, (src, dst) in enumerate((
@@ -64,40 +99,6 @@
     for copy in bring:
         copy.start()
 
-    seg, tx, ty = lax.axis_index("segment"), lax.axis_index("tx"), lax.axis_index("ty")
-    core = lax.rem(ty, 2)
-    zl = ty // 2
-    zh = lax.rem(tx, 2)
-    yy = tx // 2
-    zz = zh * 8 + zl
-
-    def at(dx, dy):
-        return (seg, lax.rem(tx + dx + NTX, NTX), lax.rem(ty + dy + NTY, NTY))
-
-    def ty_peer(q):
-        return (seg, tx, lax.rem(ty + q, NTY))
-
-    def y_peer(q):
-        return (seg, lax.rem(yy + q, NY) * 2 + zh, ty)
-
-    def z_peer(q):
-        z = lax.rem(zz + q, NZ)
-        return (seg, yy * 2 + z // 8, lax.rem(z, 8) * 2 + core)
-
-    sibling = (seg, tx, zl * 2 + 1 - core)
-    seg_next = (lax.rem(seg + 1, NSEG), tx, ty)
-    seg_prev = (lax.rem(seg + NSEG - 1, NSEG), tx, ty)
-
-    barrier = pltpu.get_barrier_semaphore()
-    around = [(1, 0), (-1, 0), (0, 1), (0, -1), (1, 1), (1, -1), (-1, 1), (-1, -1)]
-    greeted = [ty_peer(q) for q in range(1, NTY)]
-    greeted += [at(dx, dy) for dx, dy in around if dx != 0]
-    greeted += [y_peer(q) for q in range(1, NY)]
-    greeted += [z_peer(q) for q in range(1, NZ)]
-    greeted += [seg_next, seg_prev]
-    for device in greeted:
-        pl.semaphore_signal(barrier, inc=1, device_id=device, device_id_type=MESH)
-
     count = [0]
     started = []
 
@@ -111,16 +112,28 @@
             device_id=device, device_id_type=MESH,
         )
 
-    def send(src, dst, device):
+    def send(src, dst, device, goes=None, comes=None):
         copy = make(slot(), src, dst, device)
-        copy.start()
-        started.append(copy)
-        return copy
+        if goes is None:
+            copy.start()
+        else:
+            pl.when(goes)(copy.start)
+        started.append((copy, goes))
+        return copy, comes
+
+    def send_right(src, dst):
+        return send(src, dst, at(0, 1), not_right, not_left)
+
+    def send_left(src, dst):
+        return send(src, dst, at(0, -1), not_left, not_right)
 
     def arrived(name, copies):
         with jax.named_scope("await_" + name):
-            for copy in copies:
-                copy.wait_recv()
+            for copy, comes in copies:
+                if comes is None:
+                    copy.wait_recv()
+                else:
+                    pl.when(comes)(copy.wait_recv)
 
     not_top, not_bottom = tx > 0, tx < NTX - 1
     not_left, not_right = ty > 0, ty < NTY - 1
@@ -182,17 +195,16 @@
     with jax.named_scope("await_entry"):
         pl.semaphore_wait(barrier, len(greeted))
 
-    request = [send(rqs.at[q], rqr.at[q], ty_peer(q)) for q in range(1, NTY)]
-    rim = [
+    rim_tx = [
         send(srow_s, top_r, at(1, 0)),
         send(ogup_s, bot_r, at(-1, 0)),
         send(colr_s, ctl_r, at(1, 1)),
         send(coll_s, ctr_r, at(1, -1)),
         send(colr_s.at[1], cbl_r, at(-1, 1)),
         send(coll_s, cbr_r, at(-1, -1)),
-        send(colr_s, lft_r, at(0, 1)),
-        send(coll_s, rgt_r, at(0, -1)),
-    ]
+    ]
+    request = [send(rqs.at[q], rqr.at[q], ty_peer(q)) for q in range(1, NTY)]
+    rim_ty = [send_right(colr_s, lft_r), send_left(coll_s, rgt_r)]
 
     for copy in bring[6:]:
         copy.wait()
@@ -228,10 +240,6 @@
         values = keep(flag, column.astype(F32))
         plane[r, at_col : at_col + 1, :] = values[i : i + 1, :]
 
-    def put_half(value):
-        r32[0] = value[:, 0:C]
-        r32[1] = value[:, C:CP]
-
     def half_col(j):
         halves = [r32[h, pl.ds(j, H2, stride=W2), :] for h in range(2)]
         return jnp.concatenate(halves, axis=1).astype(BF)
@@ -248,6 +256,43 @@
     fill(soo, see, t32)
     fill(goo, gee, g32)
 
+    def gather_wide(first, n, lhs, row):
+        span = slice(2 * first, 2 * first + 2 * n + 2)
+        views = [goo[span, 7:39, :], gee[span, 0:32, :], goo[span, 8:40, :], gee[span, 1:33, :]]
+        for v, view in enumerate(views):
+            pairs = view.astype(BF).reshape(n + 1, 2, W2, C)
+            for u in range(4):
+                block = (u * 4 + v) * C
+                part = pairs[u // 2 : u // 2 + n, u % 2].reshape(n * W2, C)
+                lhs[row : row + n * W2, block : block + C] = part
+
+    def backward(narrow, wide):
+        pre_back = dot(narrow[...], dwp[...], ((1,), (1,)))
+        gate = jax.nn.sigmoid(pre_back)
+        raised = (pre_back * gate).astype(BF)
+        pooled = dot(wide[...], uc[...], ((1,), (1,)))
+        pre_grad = (pooled * (gate * (1.0 + pre_back * (1.0 - gate)))).astype(BF)
+        down_part = dot(narrow[...], pre_grad, ((0,), (0,)))
+        up_part = dot(raised, wide[...], ((0,), (0,)))
+        return pre_grad.astype(F32), down_part, up_part
+
+    def put_half(value, row):
+        r32[0, row : row + value.shape[0], :] = value[:, 0:C]
+        r32[1, row : row + value.shape[0], :] = value[:, C:CP]
+
+    arrived("rim_ty", rim_ty)
+    fill_col(soo, 1, 7, not_left, lft_r[0])
+    fill_col(goo, 1, 7, not_left, lft_r[1])
+    fill_col(gee, 1, W2, not_right, rgt_r[...])
+    gather_down(soo, see, 1, H2 - 2, dim, 0)
+    gather_wide(1, H2 - 2, wim, 0)
+    inner, down_part, up_part = backward(dim, wim)
+    put_half(inner, W2)
+    pgf[1 : H2 - 1, 0:W2, :] = inner.reshape(H2 - 2, W2, CP)
+    gds[0] = down_part[:, 0:C]
+    gds[1] = down_part[:, C:CP]
+    pw[...] = up_part
+
     arrived("request", request)
     wanted = jnp.concatenate([rqr[q].astype(F32) for q in range(NTY)], axis=0)
     answer = dot(wanted[:, 0:CELLS].astype(BF), coarse[...])
@@ -258,46 +303,34 @@
         send(rps.at[q], rpr.at[q], (seg, tx, lax.rem(ty + NTY - q, NTY))) for q in range(1, NTY)
     ]
 
-    arrived("rim", rim)
+    arrived("rim_tx", rim_tx)
     fill_row(soo, see, 0, not_top, top_r[0])
     fill_row(goo, gee, 0, not_top, top_r[1])
     fill_row(goo, gee, 17, not_bottom, bot_r[...])
-    fill_col(soo, 1, 7, not_left, lft_r[0])
-    fill_col(goo, 1, 7, not_left, lft_r[1])
-    fill_col(gee, 1, W2, not_right, rgt_r[...])
     fill_cell(soo, 0, 7, not_top & not_left, ctl_r[0], HT - 1)
     fill_cell(goo, 0, 7, not_top & not_left, ctl_r[1], HT - 1)
     fill_cell(gee, 0, W2, not_top & not_right, ctr_r[...], HT - 1)
     fill_cell(goo, 17, 7, not_bottom & not_left, cbl_r[...], 0)
     fill_cell(gee, 17, W2, not_bottom & not_right, cbr_r[...], 0)
-
-    gather_down(soo, see, 0, H2, dim, 0)
-    for v, view in enumerate([goo[:, 7:39, :], gee[:, 0:32, :], goo[:, 8:40, :], gee[:, 1:33, :]]):
-        view = view.astype(BF)
-        for u in range(4):
-            block = (u * 4 + v) * C
-            wim[:, block : block + C] = rows_of(view, u)
-
-    pre_back = dot(dim[...], dwp[...], ((1,), (1,)))
-    gate = jax.nn.sigmoid(pre_back)
-    prb[...] = (pre_back * gate).astype(BF)
-    pooled = dot(wim[...], uc[...], ((1,), (1,)))
-    pre_grad = (pooled * (gate * (1.0 + pre_back * (1.0 - gate)))).astype(BF)
-    half_grid = pre_grad.astype(F32)
-    put_half(half_grid)
-    pgrow_s[...] = half_grid[0:W2].astype(BF)
+    for first, row in ((0, 0), (H2 - 1, W2)):
+        gather_down(soo, see, first, 1, dimg, row)
+        gather_wide(first, 1, wimg, row)
+    outer, down_part, up_part = backward(dimg, wimg)
+    put_half(outer[0:W2], 0)
+    put_half(outer[W2:], M2 - W2)
+    pgrow_s[...] = outer[0:W2].astype(BF)
     pgcol_s[...] = half_col(0)
     pg_rim = [
         send(pgrow_s, pgrow_r, at(-1, 0)),
         send(pgcol_s, pgcor_r, at(-1, -1)),
-        send(pgcol_s, pgcol_r, at(0, -1)),
-    ]
-    pgf[0:H2, 0:W2, :] = half_grid.reshape(H2, W2, CP)
-
-    product = dot(dim[...], pre_grad, ((0,), (0,)))
-    gds[0] = product[:, 0:C]
-    gds[1] = product[:, C:CP]
-    pw[...] = dot(prb[...], wim[...], ((0,), (0,)))
+        send_left(pgcol_s, pgcol_r),
+    ]
+    pgf[0, 0:W2, :] = outer[0:W2]
+    pgf[H2 - 1, 0:W2, :] = outer[W2:]
+    gds[0] = gds[0] + down_part[:, 0:C]
+    gds[1] = gds[1] + down_part[:, C:CP]
+    pw[...] = pw[...] + up_part
+
     low = iota((ROWS // 3, C), 1) < 64
     even_lo = gds[0, pl.ds(0, ROWS // 3, stride=2), :]
     even_hi = gds[1, pl.ds(0, ROWS // 3, stride=2), :]
@@ -322,7 +355,7 @@
     arrived("swap", [swap])
     gs[...] = gf[core] + ra[...].astype(F32)
     yb[...] = gs[...].astype(BF).reshape(NY, QUART, C)
-    y_sum = [send(yb.at[lax.rem(yy + q, NY)], ry.at[q - 1], y_peer(q)) for q in range(1, NY)]
+    y_sum = [send(yb.at[lax.rem(yy + q, NY)], ry.at[q - 1], y_peer(q)) for q in (2, 1, 3)]
 
     arrived("reply", reply)
     table = jnp.concatenate([rpr[q].astype(F32) for q in range(NTY)], axis=0).astype(BF)
@@ -348,65 +381,8 @@
         send(bicol_s, bicor_r, at(1, 1)),
         send(bicol_s, bibl_r, at(-1, 1)),
     ]
-    bi_ty = [send(bicol_s, bicol_r, at(0, 1))]
+    bi_ty = [send_right(bicol_s, bicol_r)]
     fill(boo, bee, b32)
-
-    arrived("pg_rim", pg_rim)
-    pgf[H2, 0:W2, :] = keep(not_bottom, pgrow_r[...].astype(F32))
-    fill_col(pgf, 0, W2, not_right, pgcol_r[...])
-    fill_cell(pgf, H2, W2, not_bottom & not_right, pgcor_r[...], 0)
-    shifted = [
-        [pgf[di : di + H2, dj : dj + W2, :].astype(BF).reshape(M2, CP) for dj in (0, 1)]
-        for di in (0, 1)
-    ]
-
-    def spread_out(value, pr, pc):
-        for i in range(H2):
-            t32[pl.ds((2 * i + pr) * WT + pc, W2, stride=2), :] = value[i * W2 : (i + 1) * W2]
-
-    for pr in range(2):
-        for pc in range(2):
-            plane = gee[:, 0:32, :] if pc == 0 else goo[:, 8:40, :]
-            value = rows_of(plane, 1 + pr)
-            for a, di in ((1, 0),) if pr == 0 else ((2, 0), (0, 1)):
-                for b, dj in ((1, 0),) if pc == 0 else ((2, 0), (0, 1)):
-                    tap = (a * 3 + b) * C
-                    value = value + dot(shifted[di][dj], dwp[:, tap : tap + C])
-            spread_out(value, pr, pc)
-    pay_ig[...] = t32[...].astype(BF)
-
-    parts = [pl.ds(3 * WT, 12 * WT), pl.ds(0, 3 * WT), pl.ds(15 * WT, WT)]
-    slots = [(slot(), slot()) for _ in parts]
-
-    def block_copies(source):
-        return [
-            (make(up, source.at[part, :], left_out.at[part, :], seg_next),
-             make(down, source.at[part, :], right_out.at[part, :], seg_prev))
-            for part, (up, down) in zip(parts, slots)
-        ]
-
-    ig_copies, out_copies = block_copies(pay_ig), block_copies(pay_out)
-
-    @pl.when(seg == NSEG - 1)
-    def _():
-        for copy, _ in ig_copies:
-            copy.start()
-
-    @pl.when(seg >= 1)
-    def _():
-        for _, copy in ig_copies:
-            copy.start()
-
-    def send_output(which):
-        @pl.when(seg <= NSEG - 2)
-        def _():
-            for k in which:
-                out_copies[k][0].start()
-
-        @pl.when(seg == 0)
-        def _():
-            for k in which:
-                out_copies[k][1].start()
 
     def reduce(lhs):
         pre_down = dot(lhs[...], dwp[...], ((1,), (1,)))
@@ -421,47 +397,40 @@
     rdb_s[...] = half_grid[M2 - 2 * W2 :].astype(BF)
     rdl_s[...] = half_col(0)
     rdr_s[...] = half_col(W2 - 1)
-    red_rim = [
+    red_tx = [
         send(rdb_s, rdt_r, at(1, 0)),
         send(rdr_s, rtl_r, at(1, 1)),
         send(rdl_s, rtr_r, at(1, -1)),
-        send(rdr_s, rdl_r, at(0, 1)),
-        send(rdl_s, rdr_r, at(0, -1)),
-    ]
+    ]
+    red_ty = [send_right(rdr_s, rdl_r), send_left(rdl_s, rdr_r)]
     rpf[2 : H2 + 1, 8:40, :] = half_grid.reshape(H2 - 1, W2, CP)
 
-    arrived("y_sum", y_sum)
-    total = gs[pl.ds(yy * QUART, QUART), :]
-    for q in range(NY - 1):
-        total = total + ry[q].astype(F32)
-    zs[0:QUART, :] = total
-    zs[QUART:, :] = jnp.zeros((zs.shape[0] - QUART, C), F32)
-    for z in range(NZ):
-        zp[z] = zs[z * PIECE : z * PIECE + PADP, :]
-    zb[...] = zp[...].astype(BF)
-    z_sum = [send(zb.at[lax.rem(zz + q, NZ)], rz.at[q - 1], z_peer(q)) for q in range(1, NZ)]
-    arrived("bi_tx", bi_tx)
-    fill_row(boo, bee, 0, not_top, birow_r[...])
-    fill_cell(boo, 0, 7, not_top & not_left, bicor_r[...], HT - 1)
-    for k in range(2):
-        fill_row(boo, bee, 17 + k, not_bottom, biup_r[k * WT : (k + 1) * WT, :])
-        fill_cell(boo, 17 + k, 7, not_bottom & not_left, bibl_r[...], k)
-    gather_down(boo, bee, 0, 1, dimg, 0)
-    gather_down(boo, bee, H2, 1, dimg, W2)
-    half_grid = reduce(dimg)
-    upper = iota((8, CP), 0) == 0
-    rel_s[...] = jnp.where(upper, half_grid[0:1], half_grid[W2 : W2 + 1]).astype(BF)
-    rer_s[...] = jnp.where(upper, half_grid[W2 - 1 : W2], half_grid[2 * W2 - 1 :]).astype(BF)
-    red_late = [send(rer_s, rel_r, at(0, 1)), send(rel_s, rer_r, at(0, -1))]
-    rpf[1, 8:40, :] = half_grid[0:W2]
-    rpf[H2 + 1, 8:40, :] = keep(not_bottom, half_grid[W2:])
-
-    arrived("red_rim", red_rim)
-    rpf[0, 8:40, :] = keep(not_top, rdt_r[...].astype(F32))
+    parts = [pl.ds(3 * WT, 12 * WT), pl.ds(0, 3 * WT), pl.ds(15 * WT, WT)]
+    slots = [(slot(), slot()) for _ in parts]
+
+    def block_copies(source):
+        return [
+            (make(up, source.at[part, :], left_out.at[part, :], seg_next),
+             make(down, source.at[part, :], right_out.at[part, :], seg_prev))
+            for part, (up, down) in zip(parts, slots)
+        ]
+
+    ig_copies, out_copies = block_copies(pay_ig), block_copies(pay_out)
+
+    def send_output(which):
+        @pl.when(seg <= NSEG - 2)
+        def _():
+            for k in which:
+                out_copies[k][0].start()
+
+        @pl.when(seg == 0)
+        def _():
+            for k in which:
+                out_copies[k][1].start()
+
+    arrived("red_ty", red_ty)
     fill_col(rpf, 1, 7, not_left, rdl_r[...])
     fill_col(rpf, 1, 40, not_right, rdr_r[...])
-    fill_cell(rpf, 0, 7, not_top & not_left, rtl_r[...], H2 - 1)
-    fill_cell(rpf, 0, 40, not_top & not_right, rtr_r[...], H2 - 1)
     meets = (((0, 3), (1, 1)), ((1, 2), (2, 0)))
 
     def output_rows(pr, first, n):
@@ -483,6 +452,70 @@
     output_rows(1, 1, 6)
     pay_out[3 * WT : 15 * WT, :] = t32[3 * WT : 15 * WT, :].astype(BF)
     send_output((0,))
+    arrived("y_sum", y_sum)
+    total = gs[pl.ds(yy * QUART, QUART), :]
+    for q in range(NY - 1):
+        total = total + ry[q].astype(F32)
+    zs[0:QUART, :] = total
+    zs[QUART:, :] = jnp.zeros((zs.shape[0] - QUART, C), F32)
+    for z in range(NZ):
+        zp[z] = zs[z * PIECE : z * PIECE + PADP, :]
+    zb[...] = zp[...].astype(BF)
+    z_sum = [send(zb.at[lax.rem(zz + q, NZ)], rz.at[q - 1], z_peer(q)) for q in FAR_FIRST]
+    arrived("pg_rim", pg_rim)
+    pgf[H2, 0:W2, :] = keep(not_bottom, pgrow_r[...].astype(F32))
+    fill_col(pgf, 0, W2, not_right, pgcol_r[...])
+    fill_cell(pgf, H2, W2, not_bottom & not_right, pgcor_r[...], 0)
+    shifted = [
+        [pgf[di : di + H2, dj : dj + W2, :].astype(BF).reshape(M2, CP) for dj in (0, 1)]
+        for di in (0, 1)
+    ]
+
+    def spread_out(value, pr, pc):
+        for i in range(H2):
+            t32[pl.ds((2 * i + pr) * WT + pc, W2, stride=2), :] = value[i * W2 : (i + 1) * W2]
+
+    for pr in range(2):
+        for pc in range(2):
+            plane = gee[:, 0:32, :] if pc == 0 else goo[:, 8:40, :]
+            value = rows_of(plane, 1 + pr)
+            for a, di in ((1, 0),) if pr == 0 else ((2, 0), (0, 1)):
+                for b, dj in ((1, 0),) if pc == 0 else ((2, 0), (0, 1)):
+                    tap = (a * 3 + b) * C
+                    value = value + dot(shifted[di][dj], dwp[:, tap : tap + C])
+            spread_out(value, pr, pc)
+    pay_ig[...] = t32[...].astype(BF)
+
+    @pl.when(seg == NSEG - 1)
+    def _():
+        for copy, _ in ig_copies:
+            copy.start()
+
+    @pl.when(seg >= 1)
+    def _():
+        for _, copy in ig_copies:
+            copy.start()
+
+    arrived("bi_tx", bi_tx)
+    fill_row(boo, bee, 0, not_top, birow_r[...])
+    fill_cell(boo, 0, 7, not_top & not_left, bicor_r[...], HT - 1)
+    for k in range(2):
+        fill_row(boo, bee, 17 + k, not_bottom, biup_r[k * WT : (k + 1) * WT, :])
+        fill_cell(boo, 17 + k, 7, not_bottom & not_left, bibl_r[...], k)
+    gather_down(boo, bee, 0, 1, dimh, 0)
+    gather_down(boo, bee, H2, 1, dimh, W2)
+    half_grid = reduce(dimh)
+    upper = iota((8, CP), 0) == 0
+    rel_s[...] = jnp.where(upper, half_grid[0:1], half_grid[W2 : W2 + 1]).astype(BF)
+    rer_s[...] = jnp.where(upper, half_grid[W2 - 1 : W2], half_grid[2 * W2 - 1 :]).astype(BF)
+    red_late = [send_right(rer_s, rel_r), send_left(rel_s, rer_r)]
+    rpf[1, 8:40, :] = half_grid[0:W2]
+    rpf[H2 + 1, 8:40, :] = keep(not_bottom, half_grid[W2:])
+
+    arrived("red_tx", red_tx)
+    rpf[0, 8:40, :] = keep(not_top, rdt_r[...].astype(F32))
+    fill_cell(rpf, 0, 7, not_top & not_left, rtl_r[...], H2 - 1)
+    fill_cell(rpf, 0, 40, not_top & not_right, rtr_r[...], H2 - 1)
     arrived("red_late", red_late)
     for column, flag, got in ((7, not_left, rel_r), (40, not_right, rer_r)):
         fill_cell(rpf, 1, column, flag, got[...], 0)
@@ -520,8 +553,11 @@
     for pair in out_copies:
         for copy in pair:
             copy.wait_send()
-    for copy in started:
-        copy.wait_send()
+    for copy, goes in started:
+        if goes is None:
+            copy.wait_send()
+        else:
+            pl.when(goes)(copy.wait_send)
 
 
 def finish(left_h, right_h, down_h, up_h, act_o, grad_o, partner_o, down_o, up_o,
@@ -594,8 +630,9 @@
         vm((fine_rows, C), F32),
         vm((18, 40, C), F32), vm((18, 40, C), F32), vm((18, 40, C), F32), vm((18, 40, C), F32),
         vm((20, 40, C), F32), vm((20, 40, C), F32),
-        vm((M2, 9 * C), BF), vm((M2 - W2, 9 * C), BF), vm((2 * W2, 9 * C), BF), vm((M2, 16 * C), BF),
-        vm((M2, CP), BF), vm((H2 + 1, 40, CP), F32), vm((H2 + 2, 48, CP), F32), vm((2, M2, C), F32),
+        vm((M2 - 2 * W2, 9 * C), BF), vm((M2 - W2, 9 * C), BF), vm((2 * W2, 9 * C), BF),
+        vm((2 * W2, 9 * C), BF), vm((M2 - 2 * W2, 16 * C), BF), vm((2 * W2, 16 * C), BF),
+        vm((H2 + 1, 40, CP), F32), vm((H2 + 2, 48, CP), F32), vm((2, M2, C), F32),
         vm((CP, 16 * C), F32), vm((2, 9 * C, C), F32), vm((2, ROWS, C), F32), vm((ROWS, C), F32),
         vm((448, C), F32), vm((NZ, PADP, C), F32), vm((PADP, C), F32),
         vm((fine_rows, C), BF), vm((fine_rows, C), BF),

time: 62.9 us -> 58.5 us (0.930)
  the two profiles are of different devices: /device:TPU:102 before, /device:TPU:1 now
where the time goes in v3:
time: 58.5 us; the launch traced here: 58.4 us
  Pallas kernels  57.7 us (99%)
  between operations  0.64 us (1%)
    pallas_call x1, Pallas kernels, whole_step(): pl.pallas_call(kernel, out_shape=(jax.ShapeDtypeStruct((fine_rows, C), BF...  55.7 us
    pallas_call x1, Pallas kernels, local(): pl.pallas_call(finish, out_shape=(block, block, block, sums, sums), in_sp...  2 us

profile of v3, /device:TPU:1, one launch (start us, length us, event | category | flops | bytes accessed | tf_op | source)
XLA Modules:
  0.0 58.4 jit_solution(5569222854883956973)
XLA Ops:
  0.6 55.7 %relay.1 = (bf16[1024,128]{1,0:T(8,128)(2,1)}, bf16[1024,128]{1,0:T(8,128)(2,1)}, f32[1,1728]{1,0:T(1,128)}, f32[1,1728]{1,0:T(1,128)}) custom-call(bf16[1024,128]{1,0:T(8,128)(2,1)} %bitcast.15, bf16[1024,128]{1,0:T(8,128)(2,1)} %bitcast.16, bf16[1024,128]{1,0:T(8,128)(2,1)} %bitcast.17, bf16[1024,128]{1,0:T(8,128)(2,1)} %bitcast.18, ...), custom_call_target="tpu_custom_call" | custom-call | tf_op jit(solution)/shard_map/relay/pallas_call | solution.py:656
  56.4 2.0 %finish.1 = (bf16[1024,128]{1,0:T(8,128)(2,1)}, bf16[1024,128]{1,0:T(8,128)(2,1)}, bf16[1024,128]{1,0:T(8,128)(2,1)}, f32[1,1728]{1,0:T(1,128)}, f32[1,1728]{1,0:T(1,128)}) custom-call(bf16[1024,128]{1,0:T(8,128)(2,1)} %get-tuple-element.14.left_h, bf16[1024,128]{1,0:T(8,128)(2,1)} %get-tuple-element.15.right_h, f32[1,1728]{1,0:T(1,128)} %get-tuple-element.16.down_h, ...), custom_call_target="tpu_custom_call" | custom-call | tf_op jit(solution)/shard_map/finish/pallas_call | solution.py:690

commit v4 on v3

--- a/solution.py
+++ b/solution.py
@@ -195,6 +195,7 @@
     with jax.named_scope("await_entry"):
         pl.semaphore_wait(barrier, len(greeted))
 
+    request = [send(rqs.at[q], rqr.at[q], ty_peer(q)) for q in range(1, NTY)]
     rim_tx = [
         send(srow_s, top_r, at(1, 0)),
         send(ogup_s, bot_r, at(-1, 0)),
@@ -203,7 +204,6 @@
         send(colr_s.at[1], cbl_r, at(-1, 1)),
         send(coll_s, cbr_r, at(-1, -1)),
     ]
-    request = [send(rqs.at[q], rqr.at[q], ty_peer(q)) for q in range(1, NTY)]
     rim_ty = [send_right(colr_s, lft_r), send_left(coll_s, rgt_r)]
 
     for copy in bring[6:]:

time: 58.5 us -> 58.5 us (level)
  the two profiles are of different devices: /device:TPU:1 before, /device:TPU:102 now
where the time goes in v4:
time: 58.5 us; the launch traced here: 58.3 us
  Pallas kernels  57.7 us (99%)
  between operations  0.64 us (1%)
    pallas_call x1, Pallas kernels, whole_step(): pl.pallas_call(kernel, out_shape=(jax.ShapeDtypeStruct((fine_rows, C), BF...  55.7 us
    pallas_call x1, Pallas kernels, local(): pl.pallas_call(finish, out_shape=(block, block, block, sums, sums), in_sp...  2 us

profile of v4, /device:TPU:102, one launch (start us, length us, event | category | flops | bytes accessed | tf_op | source)
XLA Modules:
  0.0 58.3 jit_solution(5697168795724801107)
XLA Ops:
  0.6 55.7 %relay.1 = (bf16[1024,128]{1,0:T(8,128)(2,1)}, bf16[1024,128]{1,0:T(8,128)(2,1)}, f32[1,1728]{1,0:T(1,128)}, f32[1,1728]{1,0:T(1,128)}) custom-call(bf16[1024,128]{1,0:T(8,128)(2,1)} %bitcast.15, bf16[1024,128]{1,0:T(8,128)(2,1)} %bitcast.16, bf16[1024,128]{1,0:T(8,128)(2,1)} %bitcast.17, bf16[1024,128]{1,0:T(8,128)(2,1)} %bitcast.18, ...), custom_call_target="tpu_custom_call" | custom-call | tf_op jit(solution)/shard_map/relay/pallas_call | solution.py:656
  56.3 2.0 %finish.1 = (bf16[1024,128]{1,0:T(8,128)(2,1)}, bf16[1024,128]{1,0:T(8,128)(2,1)}, bf16[1024,128]{1,0:T(8,128)(2,1)}, f32[1,1728]{1,0:T(1,128)}, f32[1,1728]{1,0:T(1,128)}) custom-call(bf16[1024,128]{1,0:T(8,128)(2,1)} %get-tuple-element.14.left_h, bf16[1024,128]{1,0:T(8,128)(2,1)} %get-tuple-element.15.right_h, f32[1,1728]{1,0:T(1,128)} %get-tuple-element.16.down_h, ...), custom_call_target="tpu_custom_call" | custom-call | tf_op jit(solution)/shard_map/finish/pallas_call | solution.py:690
